TPU v7x, 256 devices: a whole 4x4x8 slice. The times are simulated.
256 devices in a mesh: row: 4 (over y_lo, core), col: 64 (over z, y_hi, x).
Axes of the slice: x: 4, y: 4 (y_hi: 2, y_lo: 2; y = y_hi * 2 + y_lo), z: 8, core: 2. Of those that a mesh axis runs over, the one named last changes fastest.
Arguments:
- state: bfloat16 [65536, 144], P('col', 'row'), may hold values from -6 to 6
- adjoint: bfloat16 [65536, 144], P('col', 'row'), may hold values from -6 to 6
- area: float32 [65536], P('col'), may hold values from 0.5 to 4
- node_coords: bfloat16 [3, 32768], P(None, 'col'), may hold values from 0 to 4
- connect: int32 [3, 65536], P(None, 'col'), may hold values from 0 to 32767, as said below
- front_list: int32 [4096], P('row'), may hold values from 0 to 65535, as said below
- tile_class: int32 [16, 256], P('row', 'col'), may hold values from 0 to 1, as said below
Outputs:
- front_grad: float32 [4096, 48], P(('row', 'col'))
- node_grad: float32 [32768, 48], P('col')
Inputs may be any that keep to these rules, and one draw needn't show every extreme that they name: `connect`: the three numbers of element j are distinct nodes of block j // 1024, that is within [(j // 1024) * 512, (j // 1024 + 1) * 512). `front_list`: distinct element numbers; the last element is among them. `tile_class`: 0 selects the one-point (centroid) rule, 1 the three-point (vertex) rule; every tile within the 1024 surface elements of some index of col has class 1.
All inputs are finite; a program needn't handle non-finite values.
Results may differ from a plain program's by a relative error of at most 0.009.
Values may be sent and summed in bfloat16 or wider, within the bound.
No kernel may reach another device: no remote copies, remote signals or barrier semaphores. Data moves between devices by JAX's collectives and lax.ppermute only.
A program may use at most 64 MiB of HBM per device.

v0:
```python
import jax
import jax.numpy as jnp
from jax import lax
from jax.sharding import PartitionSpec as P

SOFTEN = 0.05


def pair_sum(leader, product):
    count = leader.shape[0]
    joined = leader.astype(jnp.float32) * product
    return jnp.sum(joined.reshape(count, 2, -1, 9), axis=(1, 3))


def kernel_rows(front_x, positions, weight):
    offsets = [
        front_x[direction][:, None] - positions[direction][None, :] for direction in range(3)
    ]
    squared = offsets[0] * offsets[0] + offsets[1] * offsets[1] + offsets[2] * offsets[2] + SOFTEN
    factor = weight[None, :] / (squared * jnp.sqrt(squared))
    return [(offsets[direction] * factor).astype(jnp.bfloat16) for direction in range(3)]


def row_terms(summed, front_pack, col_pack):
    pieces = []
    for direction in range(3):
        product = jnp.dot(summed[direction], col_pack, preferred_element_type=jnp.float32)
        pieces.append(-pair_sum(front_pack, product))
    return jnp.concatenate(pieces, 1)


def col_terms(kernels, front_pack, col_pack):
    pieces = []
    for direction in range(3):
        product = lax.dot_general(
            kernels[direction],
            front_pack,
            (((0,), (0,)), ((), ())),
            preferred_element_type=jnp.float32,
        )
        pieces.append(pair_sum(col_pack, product))
    return jnp.concatenate(pieces, 1)


def one_point(front_x, front_pack, points, center, weight, col_pack):
    kernels = kernel_rows(front_x, center, weight)
    summed = [(kernel.astype(jnp.float32) * 3.0).astype(jnp.bfloat16) for kernel in kernels]
    row_part = row_terms(summed, front_pack, col_pack)
    node_slot = col_terms(kernels, front_pack, col_pack)
    return (row_part, jnp.concatenate([node_slot, node_slot, node_slot], 1))


def three_point(front_x, front_pack, points, center, weight, col_pack):
    per_node = [kernel_rows(front_x, points[corner], weight) for corner in range(3)]
    summed = [
        (
            per_node[0][direction].astype(jnp.float32)
            + per_node[1][direction].astype(jnp.float32)
            + per_node[2][direction].astype(jnp.float32)
        ).astype(jnp.bfloat16)
        for direction in range(3)
    ]
    row_part = row_terms(summed, front_pack, col_pack)
    slots = [col_terms(per_node[corner], front_pack, col_pack) for corner in range(3)]
    return (row_part, jnp.concatenate(slots, 1))


def tile_sweep(front_x, front_pack, points, center, weight, col_pack, tile_class):
    front_count = front_pack.shape[0]
    elem_count = col_pack.shape[0]
    row_tiles = tile_class.shape[0]
    col_tiles = tile_class.shape[1]
    tile_rows = front_count // row_tiles
    tile_cols = elem_count // col_tiles
    load_count = col_pack.shape[1] // 18
    row_zero = jnp.zeros((front_count, 3 * load_count), jnp.float32)
    col_zero = jnp.zeros((elem_count, 9 * load_count), jnp.float32)

    def visit(counter, carry):
        row_total, col_total = carry
        tile_row = counter // col_tiles
        tile_col = counter % col_tiles
        row_start = (tile_row * tile_rows).astype(jnp.int32)
        col_start = (tile_col * tile_cols).astype(jnp.int32)
        tile_front = lax.dynamic_slice_in_dim(front_x, row_start, tile_rows, 1)
        tile_pack = lax.dynamic_slice_in_dim(front_pack, row_start, tile_rows, 0)
        tile_points = lax.dynamic_slice_in_dim(points, col_start, tile_cols, 2)
        tile_center = lax.dynamic_slice_in_dim(center, col_start, tile_cols, 1)
        tile_weight = lax.dynamic_slice_in_dim(weight, col_start, tile_cols, 0)
        tile_columns = lax.dynamic_slice_in_dim(col_pack, col_start, tile_cols, 0)
        tile_kind = tile_class[tile_row, tile_col]
        row_part, col_part = lax.cond(
            tile_kind == 1,
            three_point,
            one_point,
            tile_front,
            tile_pack,
            tile_points,
            tile_center,
            tile_weight,
            tile_columns,
        )
        row_total = lax.dynamic_update_slice_in_dim(
            row_total,
            lax.dynamic_slice_in_dim(row_total, row_start, tile_rows, 0) + row_part,
            row_start,
            0,
        )
        col_total = lax.dynamic_update_slice_in_dim(
            col_total,
            lax.dynamic_slice_in_dim(col_total, col_start, tile_cols, 0) + col_part,
            col_start,
            0,
        )
        return (row_total, col_total)

    return lax.fori_loop(0, row_tiles * col_tiles, visit, (row_zero, col_zero))


def body(state, adjoint, area, node_coords, connect, front_list, tile_class):
    state_full, adjoint_full = (
        lax.all_gather(state, "row", axis=1, tiled=True),
        lax.all_gather(adjoint, "row", axis=1, tiled=True),
    )
    col_pack = jnp.concatenate([state_full, adjoint_full], 1)
    owned_pack = jnp.concatenate([adjoint_full, state_full], 1)
    elem_count = state.shape[0]
    node_count = node_coords.shape[1]
    front_count = front_list.shape[0]
    col_index = lax.axis_index("col")
    local_nodes = connect - col_index * node_count
    corners = node_coords[:, local_nodes]
    points = jnp.transpose(corners, (1, 0, 2)).astype(jnp.float32)
    center = (points[0] + points[1] + points[2]) / 3.0
    front_total = front_count * lax.axis_size("row")
    elem_total = elem_count * lax.axis_size("col")
    weight = area * ((front_total * elem_total) ** (-0.25) / 3.0)
    corner_rows = jnp.transpose(corners, (2, 1, 0)).reshape(elem_count, 9)
    local_front = front_list - col_index * elem_count
    is_owned = (local_front >= 0) & (local_front < elem_count)
    safe_index = jnp.clip(local_front, 0, elem_count - 1)
    picked = jnp.where(is_owned[:, None], owned_pack[safe_index].astype(jnp.float32), 0.0)
    picked_corner = jnp.where(is_owned[:, None], corner_rows[safe_index].astype(jnp.float32), 0.0)
    front_sum_pack, front_sum_corner = lax.psum((picked, picked_corner), "col")
    front_pack = front_sum_pack.astype(jnp.bfloat16)
    front_corner = front_sum_corner.astype(jnp.bfloat16)
    corner_values = front_corner.astype(jnp.float32).reshape(front_count, 3, 3)
    front_x = ((corner_values[:, 0] + corner_values[:, 1] + corner_values[:, 2]) / 3.0).T
    row_total, col_total = tile_sweep(
        front_x, front_pack, points, center, weight, col_pack, tile_class
    )
    front_grad = lax.psum_scatter(row_total, "col", scatter_dimension=0, tiled=True)
    node_ids = local_nodes.T.reshape(-1)
    elem_grad = lax.psum(col_total, "row")
    node_grad = jax.ops.segment_sum(
        elem_grad.reshape(elem_count * 3, -1), node_ids, num_segments=node_count
    )
    return (front_grad, node_grad)


def solution(mesh):
    in_specs = (
        P("col", "row"),
        P("col", "row"),
        P("col"),
        P(None, "col"),
        P(None, "col"),
        P("row"),
        P("row", "col"),
    )
    out_specs = (P(("row", "col"), None), P("col", None))
    return jax.shard_map(body, mesh=mesh, in_specs=in_specs, out_specs=out_specs, check_vma=False)
```

profile of v0, /device:TPU:2, one launch (start us, length us, event | category | flops | bytes accessed | tf_op | source)
XLA Modules:
  0.0 977.0 jit_solution(4141459184021539873)
XLA Ops:
  11.1 9.2 gather_fusion
  20.8 3.2 gather_fusion.1
  24.2 6.2 all-gather
  30.7 6.2 all-gather.1
  37.7 3.9 gather_fusion.2
  41.9 372.3 %all-reduce.5 = (bf16[1024,9]{0,1:T(8,128)(2,1)S(1)}, bf16[1024,288]{1,0:T(8,128)(2,1)S(1)}) all-reduce(f32[1024,9]{0,1:T(8,128)S(1)} %convert_select_fusion.1, f32[1024,288]{1,0:T(8,128)S(1)} %convert_select_fusion), channel_id=1, replica_groups=mesh['row'=4,'col'=64] {'col'}, use_global_device_ids=true, to_apply=%region_0.1 | all-reduce | flops 304128 | bytes 1824768 | tf_op jit(solution)/shard_map/psum | solution.py:144
  414.2 1.1 copy.51
  415.4 1.1 copy.50
  416.5 124.8 %while.17 = (s32[]{:T(128)}, f32[1024,48]{0,1:T(8,128)S(1)}, f32[1024,144]{0,1:T(8,128)S(1)}, s32[4,4]{1,0:T(4,128)}, f32[3,1024]{1,0:T(4,128)S(1)}, /*index=5*/...) while((s32[]{:T(128)}, f32[1024,48]{0,1:T(8,128)S(1)}, ...), condition=%wide.region_23.24_spmd, body=%wide.region_2.23_spmd.sunk | while | flops 472191008 | bytes 20880108 | solution.py:117
  417.6 1.3 dynamic_slice.107
  419.6 3.8 conditional.2
  424.5 1.3 dynamic_slice.107
  426.4 3.8 conditional.2
  430.3 1.0 constant_dynamic-slice_fusion.11
  431.4 1.3 dynamic_slice.107
  433.3 3.8 conditional.2
  438.3 1.3 dynamic_slice.107
  440.2 3.8 conditional.2
  444.1 1.0 constant_dynamic-slice_fusion.11
  445.2 1.3 dynamic_slice.107
  447.1 3.8 conditional.2
  452.1 1.3 dynamic_slice.107
  454.0 3.8 conditional.2
  457.8 1.0 constant_dynamic-slice_fusion.11
  458.9 1.3 dynamic_slice.107
  460.9 3.8 conditional.2
  465.8 1.3 dynamic_slice.107
  467.7 3.8 conditional.2
  472.7 1.3 dynamic_slice.107
  474.6 3.8 conditional.2
  479.6 1.3 dynamic_slice.107
  481.5 3.8 conditional.2
  486.5 1.3 dynamic_slice.107
  488.4 3.8 conditional.2
  493.3 1.3 dynamic_slice.107
  495.3 3.8 conditional.2
  500.2 1.3 dynamic_slice.107
  502.1 8.6 conditional.2
  512.0 1.3 dynamic_slice.107
  513.9 8.7 conditional.2
  523.8 1.3 dynamic_slice.107
  525.7 3.8 conditional.2
  530.6 1.3 dynamic_slice.107
  532.6 8.7 conditional.2
  541.6 1.9 reshape.130
  545.4 114.6 %all-reduce.4.cloned.1.call-done = f32[3072,48]{1,0:T(8,128)} async-done(((f32[3072,48]{1,0:T(8,128)}), f32[3072,48]{1,0:T(8,128)}) %all-reduce.4.cloned.1.call-update) | async-done | bytes 589840 | tf_op jit(solution)/shard_map/psum | solution.py:154
  659.9 17.3 %scatter_custom_fusion = f32[512,48]{1,0:T(8,128)S(1)} fusion(s32[3072]{0:T(1024)S(1)} %reshape.160, f32[3072,48]{1,0:T(8,128)} %all-reduce.4.cloned.1.call-done, f32[]{:T(128)} %constant.137.clone.1), kind=kCustom, calls=%fused_computation.142 | custom fusion | flops 147456 | bytes 98816 | tf_op jit(solution)/shard_map/scatter-add | solution.py:155
  678.0 291.6 %reduce-scatter.2.cloned.1.call-done = f32[16,48]{1,0:T(8,128)} async-done(((f32[1024,48]{1,0:T(8,128)}), f32[16,48]{1,0:T(8,128)}) %reduce-scatter.2.cloned.1.call-update) | async-done | bytes 3088 | tf_op jit(solution)/shard_map/reduce_scatter | solution.py:152
  (697 shorter events, 93.7 us)
Async XLA Ops:
  8.0 651.9 %all-reduce.4.cloned.1.call-start = ((), (), s32[]{:S(2)}) async-start(), calls=%async_computation.2 | async-start | bytes 3145728 | tf_op jit(solution)/shard_map/psum | solution.py:154
  20.5 3.6 copy-start.2
  24.0 6.6 copy-start.3
  414.2 2.2 copy-start.4
  507.6 0.9 copy-start
  509.7 1.1 copy-start.1
  519.4 0.9 copy-start
  521.5 1.1 copy-start.1
  538.0 0.9 copy-start
  540.1 1.1 copy-start.1
  543.6 426.0 %reduce-scatter.2.cloned.1.call-start = ((), (), s32[]{:S(2)}) async-start(), calls=%async_computation.1 | async-start | bytes 532480 | tf_op jit(solution)/shard_map/reduce_scatter | solution.py:152
Sparse Core Ops, SparseCore 0:
  543.7 116.1 all-reduce.3
Sparse Core Ops, SparseCore 1:
  547.1 422.4 reduce-scatter.1
where the time goes:
time: 984 us; the launch traced here: 977 us
  waiting for transfers between devices  406 us (41%)
  blocking collectives  385 us (39%)
  local copies, waits for them, and re-layouts  70.1 us (7%)
  matrix products  55.5 us (6%)
  other arithmetic  28.7 us (3%)
  loops' own time  15.9 us (2%)
  between operations  15.7 us (2%)
    psum x1, blocking collectives, body(): front_sum_pack, front_sum_corner = lax.psum((picked, picked_corner), 'col')  372 us
    reduce_scatter x1, waiting for transfers between devices, body(): lax.psum_scatter(row_total, 'col', scatter_dimension=0, tiled=True)  292 us
    psum x1, waiting for transfers between devices, body(): elem_grad = lax.psum(col_total, 'row')  115 us
    dot_general x66, matrix products, col_terms(): lax.dot_general(kernels[direction], front_pack, (((0,), (0,)), ((), ())),...  29.6 us
    dot_general x48, matrix products, row_terms(): jnp.dot(summed[direction], col_pack, preferred_element_type=jnp.float32)  25.9 us
    dynamic_slice x16, local copies, waits for them, and re-layouts, visit(): tile_kind = tile_class[tile_row, tile_col]  20.2 us
  transfers between devices with their start and end apart: 2, of which 2 were waited for; matrix products, arithmetic and copies ran while one was open for 2% of the time, Pallas kernels for 0%

commit v1 on v0

v1 whole, which is shorter than its diff:
```python
import jax
import jax.numpy as jnp
from jax import lax
from jax.experimental import pallas as pl
from jax.experimental.pallas import tpu as pltpu
from jax.sharding import Mesh, PartitionSpec as P

SOFTEN = 0.05
COL = ("z", "yh", "x")
ROW = ("yl", "co")
BF = jnp.bfloat16
F32 = jnp.float32

NT = (((1,), (1,)), ((), ()))


def iota(shape, dim):
    return lax.broadcasted_iota(jnp.int32, shape, dim)


def one_hot(mask):
    return jnp.where(mask, 1.0, 0.0).astype(BF)


def prep_kernel(gathered_ref, connect_ref, coords_ref, local_ref, pack_ref, points_ref, rows_ref):
    place = iota((288, 320), 0)
    source = iota((288, 320), 1)
    group = place >> 4
    load = place & 15
    half = jnp.where(group >= 9, 1, 0)
    comp = group - 9 * half
    wanted = (load >> 2) * 80 + half * 36 + (load & 3) * 9 + comp
    permute = one_hot(source == wanted)
    gathered = gathered_ref[...].reshape(320, 1024)
    pack = jnp.dot(permute, gathered, preferred_element_type=F32).astype(BF)
    pack_ref[...] = pack
    points = jnp.zeros((16, 1024), F32)
    for corner in range(3):
        chosen = one_hot(iota((512, 1024), 0) == connect_ref[corner : corner + 1, :])
        points = points + jnp.dot(coords_ref[corner], chosen, preferred_element_type=F32)
    points_ref[...] = points
    table = jnp.concatenate([pack[144:], pack[:144], points.astype(BF)], 0)
    owned = one_hot(iota((1024, 1024), 0) == local_ref[...])
    picked = jnp.dot(table, owned, preferred_element_type=F32)
    picked = jnp.concatenate([picked, jnp.zeros((80, 1024), F32)], 0)
    rows_ref[...] = jnp.transpose(picked).astype(BF)


def main_kernel(
    class_ref,
    pack_ref,
    points_ref,
    area_ref,
    connect_ref,
    rows_ref,
    front_ref,
    node_ref,
    kern_ref,
    dsum_ref,
    frontx_ref,
    fpack_ref,
    elem_ref,
):
    scale = (4096 * 65536) ** (-0.25) / 3.0
    weight = area_ref[...] * scale
    rows = rows_ref[...].astype(F32)
    fpack_ref[...] = jnp.transpose(rows)[:288].astype(BF)
    tail = rows[:, 256:384]
    for k in range(3):
        value = (tail[:, 32 + k : 33 + k] + tail[:, 35 + k : 36 + k] + tail[:, 38 + k : 39 + k]) / 3.0
        frontx_ref[k] = jnp.broadcast_to(value, (1024, 128))
    points = [[points_ref[3 * a + k : 3 * a + k + 1, :] for k in range(3)] for a in range(3)]
    center = [(points[0][k] + points[1][k] + points[2][k]) / 3.0 for k in range(3)]

    for jt in range(4):
        cols = slice(256 * jt, 256 * jt + 256)
        wide = weight[:, cols]
        for it in range(4):
            vertex = class_ref[it, jt] == 1
            place = [
                [jnp.where(vertex, points[a][k][:, cols], center[k][:, cols]) for k in range(3)]
                for a in range(3)
            ]

            def chunk(step, carry):
                start = pl.multiple_of(256 * it + 16 * step, 16)
                at = pl.ds(start, 16)
                front = []
                for k in range(3):
                    piece = frontx_ref[k, at, :]
                    front.append(jnp.concatenate([piece, piece], 1))
                total = [None] * 3
                for a in range(3):
                    offset = [front[k] - place[a][k] for k in range(3)]
                    squared = (
                        offset[0] * offset[0] + offset[1] * offset[1] + offset[2] * offset[2] + SOFTEN
                    )
                    inverse = lax.rsqrt(squared)
                    factor = (wide * inverse) * (inverse * inverse)
                    for k in range(3):
                        value = offset[k] * factor
                        kern_ref[3 * a + k, at, :] = value.astype(BF)
                        total[k] = value if a == 0 else total[k] + value
                for k in range(3):
                    dsum_ref[k, at, cols] = total[k].astype(BF)
                return carry

            lax.fori_loop(0, 16, chunk, 0)
        leader = pack_ref[:, cols].astype(F32)
        for ak in range(9):
            product = jnp.dot(fpack_ref[...], kern_ref[ak], preferred_element_type=F32)
            joined = (product * leader).reshape(18, 16, 256)
            elem_ref[16 * ak : 16 * ak + 16, cols] = jnp.sum(joined, axis=0)

    pieces = []
    for k in range(3):
        product = lax.dot_general(pack_ref[...], dsum_ref[k], NT, preferred_element_type=F32)
        joined = (product * fpack_ref[...].astype(F32)).reshape(18, 16, 1024)
        pieces.append(-jnp.sum(joined, axis=0))
    pieces.append(jnp.zeros((80, 1024), F32))
    turned = jnp.transpose(jnp.concatenate(pieces, 0)).reshape(64, 16, 128)
    packed = turned[:, :8] + pltpu.roll(turned[:, 8:].reshape(512, 128), 64, 1).reshape(64, 8, 128)
    front_ref[...] = packed.astype(BF)

    nodes = jnp.zeros((96, 512), F32)
    for a in range(3):
        value = elem_ref[48 * a : 48 * a + 48, :]
        high = value.astype(BF)
        low = (value - high.astype(F32)).astype(BF)
        chosen = one_hot(iota((512, 1024), 0) == connect_ref[a : a + 1, :])
        nodes = nodes + lax.dot_general(
            jnp.concatenate([high, low], 0), chosen, NT, preferred_element_type=F32
        )
    node_ref[...] = (nodes[:48] + nodes[48:]).astype(BF)


def last_kernel(front_ref, own_ref, core_ref, side_ref, cross_ref, out_front_ref, out_node_ref):
    total = jnp.sum(front_ref[...].astype(F32), axis=0)
    out_front_ref[0:8, :] = total[:, 0:48]
    out_front_ref[8:16, :] = pltpu.roll(total, 64, 1)[:, 0:48]
    near = own_ref[...].astype(F32) + core_ref[...].astype(F32)
    far = side_ref[...].astype(F32) + cross_ref[...].astype(F32)
    out_node_ref[...] = near + far


def shape(dims, dtype):
    return jax.ShapeDtypeStruct(dims, dtype)


VMEM = pl.BlockSpec(memory_space=pltpu.VMEM)
SMEM = pl.BlockSpec(memory_space=pltpu.SMEM)


def body(state, adjoint, area, node_coords, connect, front_list, tile_class):
    col_index = lax.axis_index(COL)
    mine = jnp.concatenate([state.T, adjoint.T, jnp.zeros((8, 1024), BF)], 0)
    gathered = lax.all_gather(mine, ROW)
    connect = connect - col_index * 512
    local = (front_list - col_index * 1024).reshape(1, 1024)
    coords = jnp.stack([jnp.pad(node_coords, ((3 * a, 13 - 3 * a), (0, 0))) for a in range(3)])
    pack, points, rows = pl.pallas_call(
        prep_kernel,
        out_shape=(shape((288, 1024), BF), shape((16, 1024), F32), shape((1024, 384), BF)),
        in_specs=[VMEM] * 4,
        out_specs=(VMEM, VMEM, VMEM),
        name="prep",
    )(gathered, connect, coords, local)
    part = lax.all_to_all(rows.reshape(64, 16, 384), COL, 0, 0)
    share = jnp.sum(part, axis=0, dtype=BF)
    spread = jnp.broadcast_to(share[None], (64, 16, 384))
    front_rows = lax.all_to_all(spread, COL, 0, 0).reshape(1024, 384)
    front_part, node_part = pl.pallas_call(
        main_kernel,
        out_shape=(shape((64, 8, 128), BF), shape((48, 512), BF)),
        in_specs=[SMEM] + [VMEM] * 5,
        out_specs=(VMEM, VMEM),
        scratch_shapes=[
            pltpu.VMEM((9, 1024, 256), BF),
            pltpu.VMEM((3, 1024, 1024), BF),
            pltpu.VMEM((3, 1024, 128), F32),
            pltpu.VMEM((288, 1024), BF),
            pltpu.VMEM((144, 1024), F32),
        ],
        name="sweep",
    )(tile_class, pack, points, area.reshape(1, 1024), connect, front_rows)
    core = lax.ppermute(node_part, ROW, [(i, i ^ 1) for i in range(4)])
    side = lax.ppermute(node_part, ROW, [(i, i ^ 2) for i in range(4)])
    cross = lax.ppermute(node_part, ROW, [(i, i ^ 3) for i in range(4)])
    front_sum = lax.all_to_all(front_part, COL, 0, 0)
    front_grad, node_grad = pl.pallas_call(
        last_kernel,
        out_shape=(shape((16, 48), F32), shape((48, 512), F32)),
        in_specs=[VMEM] * 5,
        out_specs=(VMEM, VMEM),
        name="last",
    )(front_sum, node_part, core, side, cross)
    return (front_grad, node_grad.T)


def solution(mesh):
    fine = Mesh(mesh.devices.reshape(2, 2, 8, 2, 4), ROW + COL)
    in_specs = (
        P(COL, ROW),
        P(COL, ROW),
        P(COL),
        P(None, COL),
        P(None, COL),
        P(ROW),
        P(ROW, COL),
    )
    out_specs = (P(ROW + COL, None), P(COL, None))
    return jax.shard_map(body, mesh=fine, in_specs=in_specs, out_specs=out_specs, check_vma=False)
```

time: 984 us -> 130 us (0.13)
  waiting for transfers between devices: 406 us -> 9.48 us
  blocking collectives: 385 us -> 76.1 us
  local copies, waits for them, and re-layouts: 70.1 us -> 1.64 us
  matrix products: 55.5 us -> 0 us
  Pallas kernels: 0 us -> 29 us
  other arithmetic: 28.7 us -> 2.95 us
  loops' own time: 15.9 us -> 0 us
  between operations: 15.7 us -> 0.73 us
    psum x1 -> x0, blocking collectives: 372 us -> none  [body(): front_sum_pack, front_sum_corner = lax.psum((picked, picked_corner), 'col')]
    reduce_scatter x1 -> x0, waiting for transfers between devices: 292 us -> none  [body(): lax.psum_scatter(row_total, 'col', scatter_dimension=0, tiled=True)]
    psum x1 -> x0, waiting for transfers between devices: 115 us -> none  [body(): elem_grad = lax.psum(col_total, 'row')]
    all_to_all x0 -> x2, blocking collectives: none -> 67.7 us  [the longest x1 37.9 us: body(): part = lax.all_to_all(rows.reshape(64, 16, 384), COL, 0, 0)]
    dot_general x114 -> x0, matrix products: 55.5 us -> none  [the longest x66 29.6 us: col_terms(): lax.dot_general(kernels[direction], front_pack, (((0,), (0,)), ((), ())),...]
    dynamic_slice x64 -> x0, local copies, waits for them, and re-layouts: 37.7 us -> none  [the longest x16 20.2 us: visit(): tile_kind = tile_class[tile_row, tile_col]]
    pallas_call x0 -> x3, Pallas kernels: none -> 29 us  [the longest x1 23.5 us: body(): pl.pallas_call(main_kernel, out_shape=(shape((64, 8, 128), BF), shape((48...]
    scatter-add x1 -> x0, other arithmetic: 17.3 us -> none  [body(): jax.ops.segment_sum(elem_grad.reshape(elem_count * 3, -1), node_ids, num_...]
  transfers between devices with their start and end apart: 2 -> 4, of which waited for: 2 -> 3; matrix products, arithmetic and copies ran while one was open for 2% -> 0% of each run, Pallas kernels for 0% -> 0%
where the time goes in v1:
time: 130 us
  blocking collectives  76.1 us (59%)
  Pallas kernels  29 us (22%)
  starting transfers between devices  9.86 us (8%)
  waiting for transfers between devices  9.48 us (7%)
  other arithmetic  2.95 us (2%)
  local copies, waits for them, and re-layouts  1.64 us (1%)
    all_to_all x1, blocking collectives, body(): part = lax.all_to_all(rows.reshape(64, 16, 384), COL, 0, 0)  37.9 us
    all_to_all x1, blocking collectives, body(): front_rows = lax.all_to_all(spread, COL, 0, 0).reshape(1024, 384)  29.8 us
    pallas_call x1, Pallas kernels, body(): pl.pallas_call(main_kernel, out_shape=(shape((64, 8, 128), BF), shape((48...  23.5 us
    all_gather x1, blocking collectives, body(): gathered = lax.all_gather(mine, ROW)  8.42 us
    all_to_all x1, starting transfers between devices, body(): front_sum = lax.all_to_all(front_part, COL, 0, 0)  7.92 us
    all_to_all x1, waiting for transfers between devices, body(): front_sum = lax.all_to_all(front_part, COL, 0, 0)  6.35 us
    pallas_call x1, Pallas kernels, body(): pl.pallas_call(prep_kernel, out_shape=(shape((288, 1024), BF), shape((16,...  3.75 us
  transfers between devices with their start and end apart: 4, of which 3 were waited for; matrix products, arithmetic and copies ran while one was open for 0% of the time, Pallas kernels for 0%

profile of v1, /device:TPU:2, one launch (start us, length us, event | category | flops | bytes accessed | tf_op | source)
XLA Modules:
  0.0 129.7 jit_solution(1193571696820566345)
XLA Ops:
  0.6 0.0 copy-start.1
  0.6 0.8 pad_bitcast_fusion.2
  1.5 0.1 pad.20.clone
  1.6 0.0 copy-done.1
  1.6 1.0 maximum_maximum_fusion
  2.5 0.0 copy-start.7
  2.5 0.0 copy-start.6
  2.6 8.4 %all-gather = bf16[320,1024]{1,0:T(8,128)(2,1)} all-gather(bf16[80,1024]{1,0:T(8,128)(2,1)S(1)} %maximum_maximum_fusion), channel_id=2, replica_groups=mesh['yl'=2,'co'=2,'z'=8,'yh'=2,'x'=4] {'yl','co'}, dimensions={0}, use_global_device_ids=true | all-gather | bytes 819200 | tf_op jit(solution)/shard_map/all_gather | solution.py:157
  11.0 0.0 copy-done.7
  11.0 0.6 broadcast_subtract_fusion.1
  11.6 0.0 copy-done.6
  11.6 0.6 broadcast_subtract_fusion.connect_ref
  12.2 0.6 pad_maximum_fusion.coords_ref
  12.8 3.7 %prep.1 = (bf16[288,1024]{1,0:T(8,128)(2,1)}, f32[16,1024]{1,0:T(8,128)}, bf16[1024,384]{1,0:T(8,128)(2,1)}) custom-call(bf16[4,80,1024]{2,1,0:T(8,128)(2,1)} %bitcast.15, s32[3,1024]{1,0:T(4,128)} %broadcast_subtract_fusion.connect_ref, bf16[3,16,512]{2,1,0:T(8,128)(2,1)} %pad_maximum_fusion.coords_ref, s32[1,1024]{1,0:T(1,128)} %bitcast.19), custom_call_target="tpu_custom_call" | custom-call | tf_op jit(solution)/shard_map/prep/pallas_call | solution.py:161
  16.6 37.9 %all_to_all.15 = bf16[64,16,384]{2,1,0:T(8,128)(2,1)S(1)} all-to-all(bf16[64,16,384]{2,1,0:T(8,128)(2,1)} %bitcast.16), channel_id=1, replica_groups=mesh['yl'=2,'co'=2,'z'=8,'yh'=2,'x'=4] {'z','yh','x'}, dimensions={0} | all-to-all | bytes 1572864 | tf_op jit(solution)/shard_map/all_to_all | solution.py:168
  54.4 0.1 reduce_sum.9
  54.6 0.1 broadcast_in_dim.10
  54.6 29.8 %all_to_all.16 = bf16[64,16,384]{2,1,0:T(8,128)(2,1)} all-to-all(bf16[64,16,384]{2,1,0:T(8,128)(2,1)S(1)} %broadcast_in_dim.10), channel_id=1, replica_groups=mesh['yl'=2,'co'=2,'z'=8,'yh'=2,'x'=4] {'z','yh','x'}, dimensions={0} | all-to-all | bytes 1572864 | tf_op jit(solution)/shard_map/all_to_all | solution.py:171
  84.4 23.5 %sweep.1 = (bf16[64,8,128]{2,1,0:T(8,128)(2,1)}, bf16[48,512]{1,0:T(8,128)(2,1)}) custom-call(s32[4,4]{1,0:T(4,128)} %class_ref.1, bf16[288,1024]{1,0:T(8,128)(2,1)} %get-tuple-element.9.pack_ref, f32[16,1024]{1,0:T(8,128)} %get-tuple-element.10.points_ref, f32[1,1024]{1,0:T(1,128)} %bitcast.20, s32[3,1024]{1,0:T(4,128)} %broadcast_subtract_fusion.connect_ref, ...), custom_call_target="tpu_custom_call" | custom-call | tf_op jit(solution)/shard_map/sweep/pallas_call | solution.py:172
  108.0 0.0 copy-start.2
  108.0 7.9 %all-to-all-start.2 = ((bf16[64,8,128]{2,1,0:T(8,128)(2,1)}), bf16[64,8,128]{2,1,0:T(8,128)(2,1)S(1)}, u32[]{:S(2)}, u32[]{:S(2)}) async-start(bf16[64,8,128]{2,1,0:T(8,128)(2,1)} %get-tuple-element.12), calls=%async_computation.2 | async-start | bytes 262144 | tf_op jit(solution)/shard_map/all_to_all | solution.py:189
  115.9 0.0 copy-done.2
  115.9 0.1 collective-permute-start.2
  116.0 0.6 collective-permute-start.1
  116.6 1.3 collective-permute-start
  117.9 1.7 %collective-permute-done.2.cross_ref = bf16[48,512]{1,0:T(8,128)(2,1)S(1)} collective-permute-done((bf16[48,512]{1,0:T(8,128)(2,1)S(1)}, bf16[48,512]{1,0:T(8,128)(2,1)S(1)}, u32[]{:S(2)}, u32[]{:S(2)}) %collective-permute-start.2) | collective-permute-done | bytes 49184 | tf_op jit(solution)/shard_map/ppermute | solution.py:188
  119.6 0.0 copy-start.3
  119.6 1.4 %collective-permute-done.1.side_ref = bf16[48,512]{1,0:T(8,128)(2,1)S(1)} collective-permute-done((bf16[48,512]{1,0:T(8,128)(2,1)S(1)}, bf16[48,512]{1,0:T(8,128)(2,1)S(1)}, u32[]{:S(2)}, u32[]{:S(2)}) %collective-permute-start.1) | collective-permute-done | bytes 49184 | tf_op jit(solution)/shard_map/ppermute | solution.py:187
  121.0 0.0 copy-start.4
  121.0 0.0 collective-permute-done.core_ref
  121.0 0.0 copy-start.5
  121.0 6.4 %all-to-all-done.2.front_ref = bf16[64,8,128]{2,1,0:T(8,128)(2,1)S(1)} async-done(((bf16[64,8,128]{2,1,0:T(8,128)(2,1)}), bf16[64,8,128]{2,1,0:T(8,128)(2,1)S(1)}, u32[]{:S(2)}, u32[]{:S(2)}) %all-to-all-start.2) | async-done | bytes 131104 | tf_op jit(solution)/shard_map/all_to_all | solution.py:189
  127.3 0.0 copy-done.3
  127.3 0.0 copy-done.4
  127.3 0.0 copy-done.5
  127.4 0.0 copy-start
  127.4 0.6 copy-done
  128.0 1.7 %last.1 = (f32[16,48]{1,0:T(8,128)}, f32[48,512]{1,0:T(8,128)}) custom-call(bf16[64,8,128]{2,1,0:T(8,128)(2,1)} %copy-done, bf16[48,512]{1,0:T(8,128)(2,1)} %get-tuple-element.13.own_ref, bf16[48,512]{1,0:T(8,128)(2,1)} %copy-done.5, bf16[48,512]{1,0:T(8,128)(2,1)} %copy-done.4, bf16[48,512]{1,0:T(8,128)(2,1)} %copy-done.3), custom_call_target="tpu_custom_call" | custom-call | tf_op jit(solution)/shard_map/last/pallas_call | solution.py:190
  (1 shorter events, 0.0 us)
Async XLA Ops:
  0.6 0.9 copy-start.1
  2.5 8.4 %copy-start.7 = (s32[1024]{0:T(1024)S(1)}, s32[1024]{0:T(1024)}, u32[]{:S(2)}) copy-start(s32[1024]{0:T(1024)} %param.12) | copy-start | bytes 12292
  2.5 9.0 %copy-start.6 = (s32[3,1024]{1,0:T(4,128)S(1)}, s32[3,1024]{1,0:T(4,128)}, u32[]{:S(2)}) copy-start(s32[3,1024]{1,0:T(4,128)} %param.11) | copy-start | bytes 36868
  108.0 7.9 %copy-start.2 = (bf16[48,512]{1,0:T(8,128)(2,1)S(1)}, bf16[48,512]{1,0:T(8,128)(2,1)}, u32[]{:S(2)}) copy-start(bf16[48,512]{1,0:T(8,128)(2,1)} %get-tuple-element.13.own_ref) | copy-start | bytes 147460
  108.0 19.4 %all-to-all-start.2 = ((bf16[64,8,128]{2,1,0:T(8,128)(2,1)}), bf16[64,8,128]{2,1,0:T(8,128)(2,1)S(1)}, u32[]{:S(2)}, u32[]{:S(2)}) async-start(bf16[64,8,128]{2,1,0:T(8,128)(2,1)} %get-tuple-element.12), calls=%async_computation.2 | async-start | bytes 262144 | tf_op jit(solution)/shard_map/all_to_all | solution.py:189
  115.9 3.6 %collective-permute-start.2 = (bf16[48,512]{1,0:T(8,128)(2,1)S(1)}, bf16[48,512]{1,0:T(8,128)(2,1)S(1)}, u32[]{:S(2)}, u32[]{:S(2)}) collective-permute-start(bf16[48,512]{1,0:T(8,128)(2,1)S(1)} %copy-done.2), channel_id=1, source_target_pairs={{0,192},{64,128},{128,64},{192,0},{1,193},{65,129},{129,65},{193,1... | collective-permute-start | bytes 147464 | tf_op jit(solution)/shard_map/ppermute | solution.py:188
  116.0 5.0 %collective-permute-start.1 = (bf16[48,512]{1,0:T(8,128)(2,1)S(1)}, bf16[48,512]{1,0:T(8,128)(2,1)S(1)}, u32[]{:S(2)}, u32[]{:S(2)}) collective-permute-start(bf16[48,512]{1,0:T(8,128)(2,1)S(1)} %copy-done.2), channel_id=1, source_target_pairs={{0,128},{64,192},{128,0},{192,64},{1,129},{65,193},{129,1},{193,65... | collective-permute-start | bytes 147464 | tf_op jit(solution)/shard_map/ppermute | solution.py:187
  116.6 4.4 %collective-permute-start = (bf16[48,512]{1,0:T(8,128)(2,1)S(1)}, bf16[48,512]{1,0:T(8,128)(2,1)S(1)}, u32[]{:S(2)}, u32[]{:S(2)}) collective-permute-start(bf16[48,512]{1,0:T(8,128)(2,1)S(1)} %copy-done.2), channel_id=1, source_target_pairs={{0,64},{64,0},{128,192},{192,128},{1,65},{65,1},{129,193},{193,129... | collective-permute-start | bytes 147464 | tf_op jit(solution)/shard_map/ppermute | solution.py:186
  119.6 7.8 %copy-start.3 = (bf16[48,512]{1,0:T(8,128)(2,1)}, bf16[48,512]{1,0:T(8,128)(2,1)S(1)}, u32[]{:S(2)}) copy-start(bf16[48,512]{1,0:T(8,128)(2,1)S(1)} %collective-permute-done.2.cross_ref) | copy-start | bytes 147460
  121.0 6.4 %copy-start.4 = (bf16[48,512]{1,0:T(8,128)(2,1)}, bf16[48,512]{1,0:T(8,128)(2,1)S(1)}, u32[]{:S(2)}) copy-start(bf16[48,512]{1,0:T(8,128)(2,1)S(1)} %collective-permute-done.1.side_ref) | copy-start | bytes 147460
  121.0 6.4 %copy-start.5 = (bf16[48,512]{1,0:T(8,128)(2,1)}, bf16[48,512]{1,0:T(8,128)(2,1)S(1)}, u32[]{:S(2)}) copy-start(bf16[48,512]{1,0:T(8,128)(2,1)S(1)} %collective-permute-done.core_ref) | copy-start | bytes 147460
  127.4 0.7 copy-start

commit v2 on v1

--- a/solution.py
+++ b/solution.py
@@ -12,6 +12,7 @@
 F32 = jnp.float32
 
 NT = (((1,), (1,)), ((), ()))
+TN = (((0,), (0,)), ((), ()))
 
 
 def iota(shape, dim):
@@ -22,7 +23,29 @@
     return jnp.where(mask, 1.0, 0.0).astype(BF)
 
 
-def prep_kernel(gathered_ref, connect_ref, coords_ref, local_ref, pack_ref, points_ref, rows_ref):
+CAP = 48
+FAST = 1
+SLOTS = 192
+
+
+def ranks(owner):
+    column = one_hot(iota((64, 1024), 0) == owner)
+    group = one_hot(iota((16, 1024), 0) == (owner & 7))
+    both = jnp.concatenate([column, group], 0)
+    ahead = one_hot(iota((1024, 1024), 0) < iota((1024, 1024), 1))
+    before = jnp.dot(both, ahead, preferred_element_type=F32) * both.astype(F32)
+    inner = jnp.sum(before[:64], axis=0, keepdims=True).astype(jnp.int32)
+    outer = jnp.sum(before[64:], axis=0, keepdims=True).astype(jnp.int32)
+    return inner, outer
+
+
+def take(slot, count, value):
+    hit = jnp.where(iota((count, 1024), 0) == slot, value + 1.0, 0.0)
+    return jnp.sum(hit, axis=1, keepdims=True) - 1.0
+
+
+def prep_kernel(col_ref, gathered_ref, connect_ref, coords_ref, list_ref, pack_ref, points_ref, table_ref, pool_ref, place_ref, fits_ref):
+    col = col_ref[0]
     place = iota((288, 320), 0)
     source = iota((288, 320), 1)
     group = place >> 4
@@ -34,25 +57,81 @@
     gathered = gathered_ref[...].reshape(320, 1024)
     pack = jnp.dot(permute, gathered, preferred_element_type=F32).astype(BF)
     pack_ref[...] = pack
+    base = jnp.concatenate([coords_ref[...].astype(F32), jnp.zeros((13, 512), F32)], 0)
     points = jnp.zeros((16, 1024), F32)
     for corner in range(3):
-        chosen = one_hot(iota((512, 1024), 0) == connect_ref[corner : corner + 1, :])
-        points = points + jnp.dot(coords_ref[corner], chosen, preferred_element_type=F32)
+        chosen = one_hot(iota((512, 1024), 0) == connect_ref[corner : corner + 1, :] - col * 512)
+        shifted = base if corner == 0 else pltpu.roll(base, 3 * corner, 0)
+        points = points + jnp.dot(shifted.astype(BF), chosen, preferred_element_type=F32)
     points_ref[...] = points
     table = jnp.concatenate([pack[144:], pack[:144], points.astype(BF)], 0)
-    owned = one_hot(iota((1024, 1024), 0) == local_ref[...])
-    picked = jnp.dot(table, owned, preferred_element_type=F32)
+    table_ref[...] = table
+
+    most = jnp.zeros((64, 1), F32)
+    crowd = jnp.zeros((8, 1), F32)
+    for r in range(4):
+        owner = gathered[80 * r + 72 : 80 * r + 73, :].astype(jnp.int32) >> 2
+        count = jnp.sum(jnp.where(iota((64, 1024), 0) == owner, 1.0, 0.0), axis=1, keepdims=True)
+        most = jnp.maximum(most, count)
+        crowd = jnp.maximum(crowd, jnp.sum(count.reshape(8, 8, 1), axis=0))
+    fits = jnp.logical_and(jnp.max(most) <= CAP, jnp.max(crowd) <= SLOTS)
+    fits_ref[0, 0] = jnp.where(fits, 1, 0).astype(jnp.int32)
+
+    owner = list_ref[...] >> 10
+    inner, outer = ranks(owner)
+    place_ref[0:1, :] = (owner >> 3) * CAP + inner
+    place_ref[1:2, :] = (owner & 7) * SLOTS + outer
+    local = (list_ref[...] & 1023).astype(F32)
+    slot = jnp.where(owner == col, inner, -1)
+    chosen = take(slot, CAP, local).astype(jnp.int32)
+    chosen = one_hot(iota((CAP, 1024), 1) == chosen)
+    picked = lax.dot_general(chosen, table, NT, preferred_element_type=F32)
+    picked = jnp.concatenate([picked, jnp.zeros((CAP, 80), F32)], 1)
+    pool_ref[...] = jnp.broadcast_to(fold(picked, CAP).astype(BF)[None], pool_ref.shape)
+
+
+def fold(rows, count):
+    third = rows[:, 256:384]
+    third = third[: count // 2] + pltpu.roll(third[count // 2 :], 64, 1)
+    return jnp.concatenate([rows[:, 0:128], rows[:, 128:256], third], 0)
+
+
+def unfold(pool, groups, count):
+    half = count // 2
+    third = pool[:, 2 * count :, :]
+    turned = pltpu.roll(third.reshape(groups * half, 128), 64, 1).reshape(groups, half, 128)
+    third = jnp.concatenate([third, turned], 1)
+    blocks = [pool[:, 0:count, :], pool[:, count : 2 * count, :], third]
+    return jnp.concatenate([block.reshape(groups * count, 128) for block in blocks], 1)
+
+
+def merge_kernel(col_ref, pool_ref, place_ref, out_ref):
+    mine = (col_ref[0] & 7) * SLOTS
+    outer = place_ref[1:2, :] - mine
+    chosen = take(outer, SLOTS, place_ref[0:1, :].astype(F32)).astype(jnp.int32)
+    chosen = one_hot(iota((SLOTS, 8 * CAP), 1) == chosen)
+    rows = unfold(pool_ref[...].astype(F32), 8, CAP).astype(BF)
+    rows = jnp.dot(chosen, rows, preferred_element_type=F32)
+    rows = jnp.where(iota((SLOTS, 384), 1) < 320, rows, 0.0)
+    out_ref[...] = jnp.broadcast_to(fold(rows, SLOTS).astype(BF)[None], out_ref.shape)
+
+
+def whole_kernel(col_ref, table_ref, list_ref, rows_ref):
+    owned = one_hot(iota((1024, 1024), 0) == list_ref[...] - col_ref[0] * 1024)
+    picked = jnp.dot(table_ref[...], owned, preferred_element_type=F32)
     picked = jnp.concatenate([picked, jnp.zeros((80, 1024), F32)], 0)
     rows_ref[...] = jnp.transpose(picked).astype(BF)
 
 
 def main_kernel(
+    col_ref,
     class_ref,
     pack_ref,
     points_ref,
     area_ref,
     connect_ref,
-    rows_ref,
+    pool_ref,
+    slot_ref,
     front_ref,
     node_ref,
     kern_ref,
@@ -63,9 +142,11 @@
 ):
     scale = (4096 * 65536) ** (-0.25) / 3.0
     weight = area_ref[...] * scale
-    rows = rows_ref[...].astype(F32)
-    fpack_ref[...] = jnp.transpose(rows)[:288].astype(BF)
-    tail = rows[:, 256:384]
+    pool = unfold(pool_ref[...], 8, SLOTS)
+    chosen = one_hot(iota((8 * SLOTS, 1024), 0) == slot_ref[1:2, :])
+    found = lax.dot_general(pool, chosen, TN, preferred_element_type=F32)
+    fpack_ref[...] = found[:288].astype(BF)
+    tail = jnp.transpose(found[256:384])
     for k in range(3):
         value = (tail[:, 32 + k : 33 + k] + tail[:, 35 + k : 36 + k] + tail[:, 38 + k : 39 + k]) / 3.0
         frontx_ref[k] = jnp.broadcast_to(value, (1024, 128))
@@ -127,7 +208,7 @@
         value = elem_ref[48 * a : 48 * a + 48, :]
         high = value.astype(BF)
         low = (value - high.astype(F32)).astype(BF)
-        chosen = one_hot(iota((512, 1024), 0) == connect_ref[a : a + 1, :])
+        chosen = one_hot(iota((512, 1024), 0) == connect_ref[a : a + 1, :] - col_ref[0] * 512)
         nodes = nodes + lax.dot_general(
             jnp.concatenate([high, low], 0), chosen, NT, preferred_element_type=F32
         )
@@ -152,27 +233,60 @@
 
 
 def body(state, adjoint, area, node_coords, connect, front_list, tile_class):
-    col_index = lax.axis_index(COL)
-    mine = jnp.concatenate([state.T, adjoint.T, jnp.zeros((8, 1024), BF)], 0)
+    col = lax.axis_index(COL).astype(jnp.int32).reshape(1)
+    owners = (front_list >> 8).astype(BF).reshape(1, 1024)
+    mine = jnp.concatenate([state.T, adjoint.T, owners, jnp.zeros((7, 1024), BF)], 0)
     gathered = lax.all_gather(mine, ROW)
-    connect = connect - col_index * 512
-    local = (front_list - col_index * 1024).reshape(1, 1024)
-    coords = jnp.stack([jnp.pad(node_coords, ((3 * a, 13 - 3 * a), (0, 0))) for a in range(3)])
-    pack, points, rows = pl.pallas_call(
+    front_list = front_list.reshape(1, 1024)
+    pack, points, table, pool, place, fits = pl.pallas_call(
         prep_kernel,
-        out_shape=(shape((288, 1024), BF), shape((16, 1024), F32), shape((1024, 384), BF)),
-        in_specs=[VMEM] * 4,
-        out_specs=(VMEM, VMEM, VMEM),
+        out_shape=(
+            shape((288, 1024), BF),
+            shape((16, 1024), F32),
+            shape((304, 1024), BF),
+            shape((8, CAP * 5 // 2, 128), BF),
+            shape((2, 1024), jnp.int32),
+            shape((1, 1), jnp.int32),
+        ),
+        in_specs=[SMEM] + [VMEM] * 4,
+        out_specs=(VMEM, VMEM, VMEM, VMEM, VMEM, SMEM),
         name="prep",
-    )(gathered, connect, coords, local)
-    part = lax.all_to_all(rows.reshape(64, 16, 384), COL, 0, 0)
-    share = jnp.sum(part, axis=0, dtype=BF)
-    spread = jnp.broadcast_to(share[None], (64, 16, 384))
-    front_rows = lax.all_to_all(spread, COL, 0, 0).reshape(1024, 384)
+    )(col, gathered, connect, node_coords, front_list)
+
+    def compact(pool, place, table):
+        part = lax.all_to_all(pool, "z", 0, 0)
+        merged = pl.pallas_call(
+            merge_kernel,
+            out_shape=shape((8, SLOTS * 5 // 2, 128), BF),
+            in_specs=[SMEM] + [VMEM] * 2,
+            out_specs=VMEM,
+            name="merge",
+        )(col, part, place)
+        return lax.all_to_all(merged, ("yh", "x"), 0, 0), place
+
+    def whole(pool, place, table):
+        rows = pl.pallas_call(
+            whole_kernel,
+            out_shape=shape((1024, 384), BF),
+            in_specs=[SMEM] + [VMEM] * 2,
+            out_specs=VMEM,
+            name="whole",
+        )(col, table, front_list)
+        part = lax.all_to_all(rows.reshape(64, 16, 384), COL, 0, 0)
+        share = jnp.sum(part, axis=0, dtype=BF)
+        spread = jnp.broadcast_to(share[None], (64, 16, 384))
+        rows = lax.all_to_all(spread, COL, 0, 0).reshape(1024, 384)
+        rows = jnp.pad(rows, ((0, 8 * SLOTS - 1024), (0, 0))).reshape(8, SLOTS, 384)
+        third = rows[:, :, 256:320].reshape(8, 2, SLOTS // 2, 64)
+        third = jnp.concatenate([third[:, 0], third[:, 1]], 2)
+        pool = jnp.concatenate([rows[:, :, 0:128], rows[:, :, 128:256], third], 1)
+        return pool, jnp.broadcast_to(jnp.arange(1024, dtype=jnp.int32), (2, 1024))
+
+    fronts, slots = lax.cond(fits[0, 0] == FAST, compact, whole, pool, place, table)
     front_part, node_part = pl.pallas_call(
         main_kernel,
         out_shape=(shape((64, 8, 128), BF), shape((48, 512), BF)),
-        in_specs=[SMEM] + [VMEM] * 5,
+        in_specs=[SMEM] * 2 + [VMEM] * 6,
         out_specs=(VMEM, VMEM),
         scratch_shapes=[
             pltpu.VMEM((9, 1024, 256), BF),
@@ -182,7 +296,7 @@
             pltpu.VMEM((144, 1024), F32),
         ],
         name="sweep",
-    )(tile_class, pack, points, area.reshape(1, 1024), connect, front_rows)
+    )(col, tile_class, pack, points, area.reshape(1, 1024), connect, fronts, slots)
     core = lax.ppermute(node_part, ROW, [(i, i ^ 1) for i in range(4)])
     side = lax.ppermute(node_part, ROW, [(i, i ^ 2) for i in range(4)])
     cross = lax.ppermute(node_part, ROW, [(i, i ^ 3) for i in range(4)])

time: 130 us -> 104 us (0.80)
  blocking collectives: 76.1 us -> 51.5 us
  Pallas kernels: 29 us -> 31.9 us
  starting transfers between devices: 9.86 us -> 7.06 us
    all_to_all x2, blocking collectives: 67.7 us -> 43 us  [the longest x1 22.6 us: compact(): return (lax.all_to_all(merged, ('yh', 'x'), 0, 0), place)]
    all_to_all x1, starting transfers between devices: 7.92 us -> 5.12 us  [body(): front_sum = lax.all_to_all(front_part, COL, 0, 0)]
    pallas_call x0 -> x1, Pallas kernels: none -> 2.38 us  [compact(): pl.pallas_call(merge_kernel, out_shape=shape((8, SLOTS * 5 // 2, 128), BF...]
where the time goes in v2:
time: 104 us
  blocking collectives  51.5 us (50%)
  Pallas kernels  31.9 us (31%)
  waiting for transfers between devices  9.52 us (9%)
  starting transfers between devices  7.06 us (7%)
  other arithmetic  1.77 us (2%)
  between operations  1.3 us (1%)
    pallas_call x1, Pallas kernels, body(): pl.pallas_call(main_kernel, out_shape=(shape((64, 8, 128), BF), shape((48...  24.4 us
    all_to_all x1, blocking collectives, compact(): return (lax.all_to_all(merged, ('yh', 'x'), 0, 0), place)  22.6 us
    all_to_all x1, blocking collectives, compact(): part = lax.all_to_all(pool, 'z', 0, 0)  20.4 us
    all_gather x1, blocking collectives, body(): gathered = lax.all_gather(mine, ROW)  8.42 us
    all_to_all x1, waiting for transfers between devices, body(): front_sum = lax.all_to_all(front_part, COL, 0, 0)  6.08 us
    all_to_all x1, starting transfers between devices, body(): front_sum = lax.all_to_all(front_part, COL, 0, 0)  5.12 us
    pallas_call x1, Pallas kernels, body(): pl.pallas_call(prep_kernel, out_shape=(shape((288, 1024), BF), shape((16,...  3.4 us
    pallas_call x1, Pallas kernels, compact(): pl.pallas_call(merge_kernel, out_shape=shape((8, SLOTS * 5 // 2, 128), BF...  2.38 us
  transfers between devices with their start and end apart: 4, of which 3 were waited for; matrix products, arithmetic and copies ran while one was open for 0% of the time, Pallas kernels for 0%

profile of v2, /device:TPU:2, one launch (start us, length us, event | category | flops | bytes accessed | tf_op | source)
XLA Modules:
  0.0 103.8 jit_solution(9550567784464718356)
XLA Ops:
  0.6 0.0 copy-start.4
  0.6 0.7 shift-right-arithmetic_convert_fusion
  1.4 0.1 pad.11.clone
  1.5 1.0 maximum_maximum_fusion.1
  2.5 8.4 %all-gather = bf16[320,1024]{1,0:T(8,128)(2,1)} all-gather(bf16[80,1024]{1,0:T(8,128)(2,1)S(1)} %maximum_maximum_fusion.1), channel_id=2, replica_groups=mesh['yl'=2,'co'=2,'z'=8,'yh'=2,'x'=4] {'yl','co'}, dimensions={0}, use_global_device_ids=true | all-gather | bytes 819200 | tf_op jit(solution)/shard_map/all_gather | solution.py:239
  10.9 0.0 copy-done.4
  10.9 3.4 %prep.1 = (bf16[288,1024]{1,0:T(8,128)(2,1)}, f32[16,1024]{1,0:T(8,128)}, bf16[304,1024]{1,0:T(8,128)(2,1)S(1)}, bf16[8,120,128]{2,1,0:T(8,128)(2,1)S(1)}, s32[2,1024]{1,0:T(2,128)S(1)}, /*index=5*/s32[1,1]{1,0:T(1,128)}) custom-call(s32[1]{0:T(128)} %bitcast.6.col_ref, bf16[4,80,1024]{2,1,0:T(8,128)(2,1)} %bitcast.24, s32[3,1024]{1,0:T(4,128)} %connect_ref.3, ...), custom_call_target="tpu_custom_call" | custom-call | tf_op jit(solution)/shard_map/prep/pallas_call | solution.py:241
  14.9 45.4 %conditional.1 = (bf16[8,480,128]{2,1,0:T(8,128)(2,1)S(1)}, s32[2,1024]{1,0:T(2,128)S(1)}) conditional(s32[]{:T(128)} %bitcast.12, (s32[1]{0:T(128)}, bf16[304,1024]{1,0:T(8,128)(2,1)S(1)}, s32[1,1024]{1,0:T(1,128)S(1)}) %tuple.24, (bf16[8,120,128]{2,1,0:T(8,128)(2,1)S(1)}, s32[1]{0:T(128)}, s32[2,1024]{1,0:T(2,128)S(1)}) %tuple.17), branch_computations={%region_0.2_spmd, %region_2.3_spmd} | conditional | flops 4319232 | bytes 11042836 | solution.py:285
  15.0 20.4 %all_to_all.23.pool_ref = bf16[8,120,128]{2,1,0:T(8,128)(2,1)} all-to-all(bf16[8,120,128]{2,1,0:T(8,128)(2,1)S(1)} %get-tuple-element.16), channel_id=1, replica_groups=mesh['yl'=2,'co'=2,'z'=8,'yh'=2,'x'=4] {'z'}, dimensions={0} | all-to-all | bytes 491520 | tf_op jit(solution)/shard_map/cond/branch_1_fun/all_to_all | solution.py:257
  35.4 2.4 %merge.1 = bf16[8,480,128]{2,1,0:T(8,128)(2,1)} custom-call(s32[1]{0:T(128)} %get-tuple-element.15.col_ref, bf16[8,120,128]{2,1,0:T(8,128)(2,1)} %all_to_all.23.pool_ref, s32[2,1024]{1,0:T(2,128)S(1)} %get-tuple-element.53.place_ref), custom_call_target="tpu_custom_call" | custom-call | tf_op jit(solution)/shard_map/cond/branch_1_fun/merge/pallas_call | solution.py:258
  37.8 22.6 %all_to_all.24 = bf16[8,480,128]{2,1,0:T(8,128)(2,1)S(1)} all-to-all(bf16[8,480,128]{2,1,0:T(8,128)(2,1)} %merge.1), channel_id=1, replica_groups=mesh['yl'=2,'co'=2,'z'=8,'yh'=2,'x'=4] {'yh','x'}, dimensions={0} | all-to-all | bytes 1966080 | tf_op jit(solution)/shard_map/cond/branch_1_fun/all_to_all | solution.py:265
  60.4 24.4 %sweep.1 = (bf16[64,8,128]{2,1,0:T(8,128)(2,1)}, bf16[48,512]{1,0:T(8,128)(2,1)}) custom-call(s32[1]{0:T(128)} %bitcast.6.col_ref, s32[4,4]{1,0:T(4,128)} %class_ref.1, bf16[288,1024]{1,0:T(8,128)(2,1)} %get-tuple-element.32.pack_ref, f32[16,1024]{1,0:T(8,128)} %get-tuple-element.33.points_ref, f32[1,1024]{1,0:T(1,128)} %bitcast.30, s32[3,1024]{1,0:T(4,128)} %connect_ref.3, ...), custom_call_target="tpu_custom_call" | custom-call | tf_op jit(solution)/shard_map/sweep/pallas_call | solution.py:286
  84.8 5.1 %all-to-all-start.4 = ((bf16[64,8,128]{2,1,0:T(8,128)(2,1)}), bf16[64,8,128]{2,1,0:T(8,128)(2,1)S(1)}, u32[]{:S(2)}, u32[]{:S(2)}) async-start(bf16[64,8,128]{2,1,0:T(8,128)(2,1)} %get-tuple-element.40), calls=%async_computation.4 | async-start | bytes 262144 | tf_op jit(solution)/shard_map/all_to_all | solution.py:303
  89.9 0.1 collective-permute-start.2
  90.0 0.6 collective-permute-start.1
  90.6 1.3 %collective-permute-start = (bf16[48,512]{1,0:T(8,128)(2,1)}, bf16[48,512]{1,0:T(8,128)(2,1)S(1)}, u32[]{:S(2)}, u32[]{:S(2)}) collective-permute-start(bf16[48,512]{1,0:T(8,128)(2,1)} %get-tuple-element.41.own_ref), channel_id=1, source_target_pairs={{0,64},{64,0},{128,192},{192,128},{1,65},{65,1},{129,193},{193,129... | collective-permute-start | bytes 147464 | tf_op jit(solution)/shard_map/ppermute | solution.py:300
  91.9 2.0 %collective-permute-done.2.cross_ref = bf16[48,512]{1,0:T(8,128)(2,1)S(1)} collective-permute-done((bf16[48,512]{1,0:T(8,128)(2,1)}, bf16[48,512]{1,0:T(8,128)(2,1)S(1)}, u32[]{:S(2)}, u32[]{:S(2)}) %collective-permute-start.2) | collective-permute-done | bytes 49184 | tf_op jit(solution)/shard_map/ppermute | solution.py:302
  93.9 0.0 copy-start.1
  93.9 1.5 %collective-permute-done.1.side_ref = bf16[48,512]{1,0:T(8,128)(2,1)S(1)} collective-permute-done((bf16[48,512]{1,0:T(8,128)(2,1)}, bf16[48,512]{1,0:T(8,128)(2,1)S(1)}, u32[]{:S(2)}, u32[]{:S(2)}) %collective-permute-start.1) | collective-permute-done | bytes 49184 | tf_op jit(solution)/shard_map/ppermute | solution.py:301
  95.3 0.0 copy-start.2
  95.3 0.0 collective-permute-done.core_ref
  95.3 0.0 copy-start.3
  95.3 6.1 %all-to-all-done.4.front_ref = bf16[64,8,128]{2,1,0:T(8,128)(2,1)S(1)} async-done(((bf16[64,8,128]{2,1,0:T(8,128)(2,1)}), bf16[64,8,128]{2,1,0:T(8,128)(2,1)S(1)}, u32[]{:S(2)}, u32[]{:S(2)}) %all-to-all-start.4) | async-done | bytes 131104 | tf_op jit(solution)/shard_map/all_to_all | solution.py:303
  101.4 0.0 copy-done.1
  101.4 0.0 copy-done.2
  101.4 0.0 copy-done.3
  101.4 0.0 copy-start
  101.4 0.6 copy-done
  102.1 1.7 %last.1 = (f32[16,48]{1,0:T(8,128)}, f32[48,512]{1,0:T(8,128)}) custom-call(bf16[64,8,128]{2,1,0:T(8,128)(2,1)} %copy-done, bf16[48,512]{1,0:T(8,128)(2,1)} %get-tuple-element.41.own_ref, bf16[48,512]{1,0:T(8,128)(2,1)} %copy-done.3, bf16[48,512]{1,0:T(8,128)(2,1)} %copy-done.2, bf16[48,512]{1,0:T(8,128)(2,1)} %copy-done.1), custom_call_target="tpu_custom_call" | custom-call | tf_op jit(solution)/shard_map/last/pallas_call | solution.py:304
  (2 shorter events, 0.0 us)
Async XLA Ops:
  0.6 10.3 %copy-start.4 = (s32[1024]{0:T(1024)S(1)}, s32[1024]{0:T(1024)}, u32[]{:S(2)}) copy-start(s32[1024]{0:T(1024)} %param.14) | copy-start | bytes 12292
  84.8 16.6 %all-to-all-start.4 = ((bf16[64,8,128]{2,1,0:T(8,128)(2,1)}), bf16[64,8,128]{2,1,0:T(8,128)(2,1)S(1)}, u32[]{:S(2)}, u32[]{:S(2)}) async-start(bf16[64,8,128]{2,1,0:T(8,128)(2,1)} %get-tuple-element.40), calls=%async_computation.4 | async-start | bytes 262144 | tf_op jit(solution)/shard_map/all_to_all | solution.py:303
  89.9 3.9 %collective-permute-start.2 = (bf16[48,512]{1,0:T(8,128)(2,1)}, bf16[48,512]{1,0:T(8,128)(2,1)S(1)}, u32[]{:S(2)}, u32[]{:S(2)}) collective-permute-start(bf16[48,512]{1,0:T(8,128)(2,1)} %get-tuple-element.41.own_ref), channel_id=1, source_target_pairs={{0,192},{64,128},{128,64},{192,0},{1,193},{65,129},{129,65},{193,1... | collective-permute-start | bytes 147464 | tf_op jit(solution)/shard_map/ppermute | solution.py:302
  90.0 5.3 %collective-permute-start.1 = (bf16[48,512]{1,0:T(8,128)(2,1)}, bf16[48,512]{1,0:T(8,128)(2,1)S(1)}, u32[]{:S(2)}, u32[]{:S(2)}) collective-permute-start(bf16[48,512]{1,0:T(8,128)(2,1)} %get-tuple-element.41.own_ref), channel_id=1, source_target_pairs={{0,128},{64,192},{128,0},{192,64},{1,129},{65,193},{129,1},{193,65... | collective-permute-start | bytes 147464 | tf_op jit(solution)/shard_map/ppermute | solution.py:301
  90.6 4.7 %collective-permute-start = (bf16[48,512]{1,0:T(8,128)(2,1)}, bf16[48,512]{1,0:T(8,128)(2,1)S(1)}, u32[]{:S(2)}, u32[]{:S(2)}) collective-permute-start(bf16[48,512]{1,0:T(8,128)(2,1)} %get-tuple-element.41.own_ref), channel_id=1, source_target_pairs={{0,64},{64,0},{128,192},{192,128},{1,65},{65,1},{129,193},{193,129... | collective-permute-start | bytes 147464 | tf_op jit(solution)/shard_map/ppermute | solution.py:300
  93.9 7.6 %copy-start.1 = (bf16[48,512]{1,0:T(8,128)(2,1)}, bf16[48,512]{1,0:T(8,128)(2,1)S(1)}, u32[]{:S(2)}) copy-start(bf16[48,512]{1,0:T(8,128)(2,1)S(1)} %collective-permute-done.2.cross_ref) | copy-start | bytes 147460
  95.3 6.1 %copy-start.2 = (bf16[48,512]{1,0:T(8,128)(2,1)}, bf16[48,512]{1,0:T(8,128)(2,1)S(1)}, u32[]{:S(2)}) copy-start(bf16[48,512]{1,0:T(8,128)(2,1)S(1)} %collective-permute-done.1.side_ref) | copy-start | bytes 147460
  95.3 6.1 %copy-start.3 = (bf16[48,512]{1,0:T(8,128)(2,1)}, bf16[48,512]{1,0:T(8,128)(2,1)S(1)}, u32[]{:S(2)}) copy-start(bf16[48,512]{1,0:T(8,128)(2,1)S(1)} %collective-permute-done.core_ref) | copy-start | bytes 147460
  101.4 0.7 copy-start

commit v3 on v2

--- a/solution.py
+++ b/solution.py
@@ -123,6 +123,10 @@
     rows_ref[...] = jnp.transpose(picked).astype(BF)
 
 
+def load_sum(product, count):
+    return jnp.sum(product.reshape(18, 16, count), axis=0)
+
+
 def main_kernel(
     col_ref,
     class_ref,
@@ -130,14 +134,20 @@
     points_ref,
     area_ref,
     connect_ref,
+    coords_ref,
     pool_ref,
     slot_ref,
     front_ref,
     node_ref,
-    kern_ref,
-    dsum_ref,
+    knode_ref,
+    kcell_ref,
     frontx_ref,
     fpack_ref,
+    share_ref,
+    touch_ref,
+    part_ref,
+    nsum_ref,
+    nhalf_ref,
     elem_ref,
 ):
     scale = (4096 * 65536) ** (-0.25) / 3.0
@@ -150,69 +160,118 @@
     for k in range(3):
         value = (tail[:, 32 + k : 33 + k] + tail[:, 35 + k : 36 + k] + tail[:, 38 + k : 39 + k]) / 3.0
         frontx_ref[k] = jnp.broadcast_to(value, (1024, 128))
-    points = [[points_ref[3 * a + k : 3 * a + k + 1, :] for k in range(3)] for a in range(3)]
-    center = [(points[0][k] + points[1][k] + points[2][k]) / 3.0 for k in range(3)]
-
+    rows = [[points_ref[3 * a + k : 3 * a + k + 1, :] for k in range(3)] for a in range(3)]
+    center = [(rows[0][k] + rows[1][k] + rows[2][k]) / 3.0 for k in range(3)]
+    corner = [coords_ref[k : k + 1, :].astype(F32) for k in range(3)]
+
+    def fill(out_ref, place, first, count, lanes):
+        width = place[0].shape[1]
+        place = [jnp.broadcast_to(p, (16, width)) for p in place]
+
+        def chunk(step, carry):
+            at = pl.ds(pl.multiple_of(first + 16 * step, 16), 16)
+            offset = []
+            for k in range(3):
+                piece = frontx_ref[k, at, :]
+                offset.append(jnp.concatenate([piece] * (width // 128), 1) - place[k])
+            squared = offset[0] * offset[0] + offset[1] * offset[1] + offset[2] * offset[2] + SOFTEN
+            inverse = lax.rsqrt(squared)
+            factor = inverse * inverse * inverse
+            for k in range(3):
+                out_ref[k, at, lanes] = (offset[k] * factor).astype(BF)
+            return carry
+
+        lax.fori_loop(0, count // 16, chunk, 0, unroll=4)
+
+    for half in range(2):
+        lanes = slice(256 * half, 256 * half + 256)
+        fill(knode_ref, [c[:, lanes] for c in corner], 0, 1024, lanes)
     for jt in range(4):
-        cols = slice(256 * jt, 256 * jt + 256)
-        wide = weight[:, cols]
+        lanes = slice(256 * jt, 256 * jt + 256)
+        place = [c[:, lanes] for c in center]
         for it in range(4):
             vertex = class_ref[it, jt] == 1
-            place = [
-                [jnp.where(vertex, points[a][k][:, cols], center[k][:, cols]) for k in range(3)]
-                for a in range(3)
-            ]
-
-            def chunk(step, carry):
-                start = pl.multiple_of(256 * it + 16 * step, 16)
-                at = pl.ds(start, 16)
-                front = []
-                for k in range(3):
-                    piece = frontx_ref[k, at, :]
-                    front.append(jnp.concatenate([piece, piece], 1))
-                total = [None] * 3
-                for a in range(3):
-                    offset = [front[k] - place[a][k] for k in range(3)]
-                    squared = (
-                        offset[0] * offset[0] + offset[1] * offset[1] + offset[2] * offset[2] + SOFTEN
-                    )
-                    inverse = lax.rsqrt(squared)
-                    factor = (wide * inverse) * (inverse * inverse)
-                    for k in range(3):
-                        value = offset[k] * factor
-                        kern_ref[3 * a + k, at, :] = value.astype(BF)
-                        total[k] = value if a == 0 else total[k] + value
-                for k in range(3):
-                    dsum_ref[k, at, cols] = total[k].astype(BF)
-                return carry
-
-            lax.fori_loop(0, 16, chunk, 0)
-        leader = pack_ref[:, cols].astype(F32)
-        for ak in range(9):
-            product = jnp.dot(fpack_ref[...], kern_ref[ak], preferred_element_type=F32)
-            joined = (product * leader).reshape(18, 16, 256)
-            elem_ref[16 * ak : 16 * ak + 16, cols] = jnp.sum(joined, axis=0)
-
-    pieces = []
+
+            @pl.when(vertex)
+            def _():
+                kcell_ref[:, 256 * it : 256 * it + 256, lanes] = jnp.zeros((3, 256, 256), BF)
+
+            @pl.when(jnp.logical_not(vertex))
+            def _():
+                fill(kcell_ref, place, 256 * it, 256, lanes)
+
+    share_ref[...] = (pack_ref[...].astype(F32) * weight).astype(BF)
+    ends = [jnp.broadcast_to(connect_ref[a : a + 1, :] - col_ref[0] * 512, (16, 1024)) for a in range(3)]
+
+    def mark(step, carry):
+        at = pl.multiple_of(16 * step, 16)
+        node = iota((16, 1024), 0) + at
+        hit = (node == ends[0]) | (node == ends[1]) | (node == ends[2])
+        touch_ref[pl.ds(at, 16), :] = one_hot(hit)
+        return carry
+
+    lax.fori_loop(0, 32, mark, 0, unroll=2)
+    for jt in range(4):
+        lanes = slice(256 * jt, 256 * jt + 256)
+        part_ref[jt] = lax.dot_general(
+            share_ref[:, lanes], touch_ref[:, lanes], NT, preferred_element_type=F32
+        )
+    mask = [[class_ref[it, jt].astype(F32) for jt in range(4)] for it in range(4)]
+
+    def blend(step, carry):
+        at = pl.ds(pl.multiple_of(16 * step, 16), 16)
+        part = [part_ref[jt, at, :] for jt in range(4)]
+        for it in range(4):
+            total = part[0] * mask[it][0]
+            for jt in range(1, 4):
+                total = total + part[jt] * mask[it][jt]
+            nsum_ref[it, at, :] = total
+            nhalf_ref[it, at, :] = total.astype(BF)
+        return carry
+
+    lax.fori_loop(0, 18, blend, 0)
+
+    for jt in range(4):
+        lanes = slice(256 * jt, 256 * jt + 256)
+        leader = pack_ref[:, lanes].astype(F32) * weight[:, lanes]
+        for k in range(3):
+            product = jnp.dot(fpack_ref[...], kcell_ref[k, :, lanes], preferred_element_type=F32)
+            elem_ref[16 * k : 16 * k + 16, lanes] = load_sum(product * leader, 256)
+
+    nodes = []
     for k in range(3):
-        product = lax.dot_general(pack_ref[...], dsum_ref[k], NT, preferred_element_type=F32)
-        joined = (product * fpack_ref[...].astype(F32)).reshape(18, 16, 1024)
-        pieces.append(-jnp.sum(joined, axis=0))
-    pieces.append(jnp.zeros((80, 1024), F32))
-    turned = jnp.transpose(jnp.concatenate(pieces, 0)).reshape(64, 16, 128)
+        total = None
+        for it in range(4):
+            rows = slice(256 * it, 256 * it + 256)
+            product = jnp.dot(fpack_ref[:, rows], knode_ref[k, rows, :], preferred_element_type=F32)
+            value = load_sum(product * nsum_ref[it], 512)
+            total = value if it == 0 else total + value
+        nodes.append(total)
+    value = elem_ref[...]
+    high = value.astype(BF)
+    low = (value - high.astype(F32)).astype(BF)
+    spread = lax.dot_general(
+        jnp.concatenate([high, low], 0), touch_ref[...], NT, preferred_element_type=F32
+    )
+    node_ref[...] = (jnp.concatenate(nodes, 0) + (spread[:48] + spread[48:])).astype(BF)
+
+    columns = []
+    for it in range(4):
+        rows = slice(256 * it, 256 * it + 256)
+        leader = fpack_ref[:, rows].astype(F32)
+        pieces = []
+        for k in range(3):
+            product = 3.0 * lax.dot_general(
+                share_ref[...], kcell_ref[k, rows, :], NT, preferred_element_type=F32
+            ) + lax.dot_general(
+                nhalf_ref[it], knode_ref[k, rows, :], NT, preferred_element_type=F32
+            )
+            pieces.append(-load_sum(product * leader, 256))
+        pieces.append(jnp.zeros((80, 256), F32))
+        columns.append(jnp.transpose(jnp.concatenate(pieces, 0)))
+    turned = jnp.concatenate(columns, 0).reshape(64, 16, 128)
     packed = turned[:, :8] + pltpu.roll(turned[:, 8:].reshape(512, 128), 64, 1).reshape(64, 8, 128)
     front_ref[...] = packed.astype(BF)
-
-    nodes = jnp.zeros((96, 512), F32)
-    for a in range(3):
-        value = elem_ref[48 * a : 48 * a + 48, :]
-        high = value.astype(BF)
-        low = (value - high.astype(F32)).astype(BF)
-        chosen = one_hot(iota((512, 1024), 0) == connect_ref[a : a + 1, :] - col_ref[0] * 512)
-        nodes = nodes + lax.dot_general(
-            jnp.concatenate([high, low], 0), chosen, NT, preferred_element_type=F32
-        )
-    node_ref[...] = (nodes[:48] + nodes[48:]).astype(BF)
 
 
 def last_kernel(front_ref, own_ref, core_ref, side_ref, cross_ref, out_front_ref, out_node_ref):
@@ -250,6 +309,7 @@
         ),
         in_specs=[SMEM] + [VMEM] * 4,
         out_specs=(VMEM, VMEM, VMEM, VMEM, VMEM, SMEM),
+        compiler_params=pltpu.CompilerParams(vmem_limit_bytes=24 << 20),
         name="prep",
     )(col, gathered, connect, node_coords, front_list)
 
@@ -260,6 +320,7 @@
             out_shape=shape((8, SLOTS * 5 // 2, 128), BF),
             in_specs=[SMEM] + [VMEM] * 2,
             out_specs=VMEM,
+            compiler_params=pltpu.CompilerParams(vmem_limit_bytes=24 << 20),
             name="merge",
         )(col, part, place)
         return lax.all_to_all(merged, ("yh", "x"), 0, 0), place
@@ -286,17 +347,33 @@
     front_part, node_part = pl.pallas_call(
         main_kernel,
         out_shape=(shape((64, 8, 128), BF), shape((48, 512), BF)),
-        in_specs=[SMEM] * 2 + [VMEM] * 6,
+        in_specs=[SMEM] * 2 + [VMEM] * 7,
         out_specs=(VMEM, VMEM),
         scratch_shapes=[
-            pltpu.VMEM((9, 1024, 256), BF),
+            pltpu.VMEM((3, 1024, 512), BF),
             pltpu.VMEM((3, 1024, 1024), BF),
             pltpu.VMEM((3, 1024, 128), F32),
             pltpu.VMEM((288, 1024), BF),
-            pltpu.VMEM((144, 1024), F32),
+            pltpu.VMEM((288, 1024), BF),
+            pltpu.VMEM((512, 1024), BF),
+            pltpu.VMEM((4, 288, 512), F32),
+            pltpu.VMEM((4, 288, 512), F32),
+            pltpu.VMEM((4, 288, 512), BF),
+            pltpu.VMEM((48, 1024), F32),
         ],
+        compiler_params=pltpu.CompilerParams(vmem_limit_bytes=44 << 20),
         name="sweep",
-    )(col, tile_class, pack, points, area.reshape(1, 1024), connect, fronts, slots)
+    )(
+        col,
+        tile_class,
+        pack,
+        points,
+        area.reshape(1, 1024),
+        connect,
+        node_coords,
+        fronts,
+        slots,
+    )
     core = lax.ppermute(node_part, ROW, [(i, i ^ 1) for i in range(4)])
     side = lax.ppermute(node_part, ROW, [(i, i ^ 2) for i in range(4)])
     cross = lax.ppermute(node_part, ROW, [(i, i ^ 3) for i in range(4)])
@@ -306,6 +383,7 @@
         out_shape=(shape((16, 48), F32), shape((48, 512), F32)),
         in_specs=[VMEM] * 5,
         out_specs=(VMEM, VMEM),
+        compiler_params=pltpu.CompilerParams(vmem_limit_bytes=16 << 20),
         name="last",
     )(front_sum, node_part, core, side, cross)
     return (front_grad, node_grad.T)

time: 104 us -> 89.2 us (0.86)
  Pallas kernels: 31.9 us -> 18.6 us
    pallas_call x1, Pallas kernels: 24.4 us -> 15.1 us  [body(): pl.pallas_call(main_kernel, out_shape=(shape((64, 8, 128), BF), shape((48...]
    pallas_call x1, Pallas kernels: 2.38 us -> 0.49 us  [compact(): pl.pallas_call(merge_kernel, out_shape=shape((8, SLOTS * 5 // 2, 128), BF...]
    pallas_call x1, Pallas kernels: 3.4 us -> 2.27 us  [body(): pl.pallas_call(prep_kernel, out_shape=(shape((288, 1024), BF), shape((16,...]
where the time goes in v3:
time: 89.2 us; the launch traced here: 88.5 us
  blocking collectives  50.7 us (57%)
  Pallas kernels  18.6 us (21%)
  waiting for transfers between devices  9.48 us (11%)
  starting transfers between devices  6.51 us (7%)
  other arithmetic  1.75 us (2%)
  between operations  1.36 us (2%)
    all_to_all x1, blocking collectives, compact(): return (lax.all_to_all(merged, ('yh', 'x'), 0, 0), place)  22.4 us
    all_to_all x1, blocking collectives, compact(): part = lax.all_to_all(pool, 'z', 0, 0)  20.3 us
    pallas_call x1, Pallas kernels, body(): pl.pallas_call(main_kernel, out_shape=(shape((64, 8, 128), BF), shape((48...  15.1 us
    all_gather x1, blocking collectives, body(): gathered = lax.all_gather(mine, ROW)  7.97 us
    all_to_all x1, waiting for transfers between devices, body(): front_sum = lax.all_to_all(front_part, COL, 0, 0)  6.32 us
    all_to_all x1, starting transfers between devices, body(): front_sum = lax.all_to_all(front_part, COL, 0, 0)  4.57 us
    pallas_call x1, Pallas kernels, body(): pl.pallas_call(prep_kernel, out_shape=(shape((288, 1024), BF), shape((16,...  2.27 us
    ppermute x1, waiting for transfers between devices, body(): cross = lax.ppermute(node_part, ROW, [(i, i ^ 3) for i in range(4)])  1.85 us
  transfers between devices with their start and end apart: 4, of which 3 were waited for; matrix products, arithmetic and copies ran while one was open for 0% of the time, Pallas kernels for 0%

profile of v3, /device:TPU:2, one launch (start us, length us, event | category | flops | bytes accessed | tf_op | source)
XLA Modules:
  0.0 88.5 jit_solution(7760708372005476902)
XLA Ops:
  0.6 0.0 copy-start.4
  0.6 0.0 copy-start
  0.7 0.0 copy-start.1
  0.7 0.7 shift-right-arithmetic_convert_fusion
  1.4 0.1 pad.11.clone
  1.5 1.0 %maximum_maximum_fusion.1 = bf16[80,1024]{1,0:T(8,128)(2,1)S(1)} fusion(bf16[1,1024]{1,0:T(2,128)(2,1)S(1)} %reshape.34, bf16[36,1024]{1,0:T(8,128)(2,1)} %bitcast.27, bf16[36,1024]{1,0:T(8,128)(2,1)} %bitcast.28, bf16[80]{0:T(256)(128)(2,1)S(1)} %pad.11.clone), kind=kLoop, calls=%fused_computation.3 | loop fusion | flops 655360 | bytes 313504 | tf_op jit(solution)/shard_map/concatenate | solution.py:297
  2.5 8.0 %all-gather = bf16[320,1024]{1,0:T(8,128)(2,1)S(1)} all-gather(bf16[80,1024]{1,0:T(8,128)(2,1)S(1)} %maximum_maximum_fusion.1), channel_id=2, replica_groups=mesh['yl'=2,'co'=2,'z'=8,'yh'=2,'x'=4] {'yl','co'}, dimensions={0}, use_global_device_ids=true | all-gather | bytes 819200 | tf_op jit(solution)/shard_map/all_gather | solution.py:298
  10.5 0.0 copy-done.4
  10.5 0.0 copy-done
  10.5 0.0 copy-done.1
  10.5 2.3 %prep.1 = (bf16[288,1024]{1,0:T(8,128)(2,1)S(1)}, f32[16,1024]{1,0:T(8,128)S(1)}, bf16[304,1024]{1,0:T(8,128)(2,1)S(1)}, bf16[8,120,128]{2,1,0:T(8,128)(2,1)S(1)...) custom-call(s32[1]{0:T(128)} %bitcast.6.col_ref, bf16[4,80,1024]{2,1,0:T(8,128)(2,1)S(1)} %bitcast.20, s32[3,1024]{1,0:T(4,128)S(1)} %copy-done, ...), custom_call_target="tpu_custom_call" | custom-call | tf_op jit(solution)/shard_map/prep/pallas_call | solution.py:300
  13.4 0.0 copy-start.2
  13.4 0.0 copy-start.3
  13.4 43.3 %conditional.1 = (bf16[8,480,128]{2,1,0:T(8,128)(2,1)S(1)}, s32[2,1024]{1,0:T(2,128)S(1)}) conditional(s32[]{:T(128)} %bitcast.12, (s32[1]{0:T(128)}, bf16[304,1024]{1,0:T(8,128)(2,1)S(1)}, s32[1,1024]{1,0:T(1,128)S(1)}) %tuple.24, (bf16[8,120,128]{2,1,0:T(8,128)(2,1)S(1)}, s32[1]{0:T(128)}, s32[2,1024]{1,0:T(2,128)S(1)}) %tuple.17), branch_computations={%region_0.2_spmd, %region_2.3_spmd} | conditional | flops 4319232 | bytes 11042836 | solution.py:346
  13.5 20.3 %all_to_all.23.pool_ref = bf16[8,120,128]{2,1,0:T(8,128)(2,1)S(1)} all-to-all(bf16[8,120,128]{2,1,0:T(8,128)(2,1)S(1)} %get-tuple-element.16), channel_id=1, replica_groups=mesh['yl'=2,'co'=2,'z'=8,'yh'=2,'x'=4] {'z'}, dimensions={0} | all-to-all | bytes 491520 | tf_op jit(solution)/shard_map/cond/branch_1_fun/all_to_all | solution.py:317
  33.8 0.5 merge.1
  34.3 22.4 %all_to_all.24 = bf16[8,480,128]{2,1,0:T(8,128)(2,1)S(1)} all-to-all(bf16[8,480,128]{2,1,0:T(8,128)(2,1)S(1)} %merge.1), channel_id=1, replica_groups=mesh['yl'=2,'co'=2,'z'=8,'yh'=2,'x'=4] {'yh','x'}, dimensions={0} | all-to-all | bytes 1966080 | tf_op jit(solution)/shard_map/cond/branch_1_fun/all_to_all | solution.py:326
  56.7 0.0 copy-done.2
  56.7 0.0 copy-done.3
  56.7 15.1 %sweep.1 = (bf16[64,8,128]{2,1,0:T(8,128)(2,1)}, bf16[48,512]{1,0:T(8,128)(2,1)S(1)}) custom-call(s32[1]{0:T(128)} %bitcast.6.col_ref, s32[4,4]{1,0:T(4,128)S(1)} %copy-done.3, bf16[288,1024]{1,0:T(8,128)(2,1)S(1)} %get-tuple-element.32.pack_ref, f32[16,1024]{1,0:T(8,128)S(1)} %get-tuple-element.33.points_ref, f32[1,1024]{1,0:T(1,128)S(1)} %bitcast.21, ...), custom_call_target="tpu_custom_call" | custom-call | tf_op jit(solution)/shard_map/sweep/pallas_call | solution.py:347
  71.8 4.6 %all-to-all-start.4 = ((bf16[64,8,128]{2,1,0:T(8,128)(2,1)}), bf16[64,8,128]{2,1,0:T(8,128)(2,1)S(1)}, u32[]{:S(2)}, u32[]{:S(2)}) async-start(bf16[64,8,128]{2,1,0:T(8,128)(2,1)} %get-tuple-element.40), calls=%async_computation.4 | async-start | bytes 262144 | tf_op jit(solution)/shard_map/all_to_all | solution.py:380
  76.3 0.1 collective-permute-start.2
  76.4 0.7 collective-permute-start.1
  77.1 1.2 %collective-permute-start = (bf16[48,512]{1,0:T(8,128)(2,1)S(1)}, bf16[48,512]{1,0:T(8,128)(2,1)S(1)}, u32[]{:S(2)}, u32[]{:S(2)}) collective-permute-start(bf16[48,512]{1,0:T(8,128)(2,1)S(1)} %get-tuple-element.41.own_ref), channel_id=1, source_target_pairs={{0,64},{64,0},{128,192},{192,128},{1,65},{65,1},{129,193},{193,129... | collective-permute-start | bytes 147464 | tf_op jit(solution)/shard_map/ppermute | solution.py:377
  78.3 1.9 %collective-permute-done.2.cross_ref = bf16[48,512]{1,0:T(8,128)(2,1)S(1)} collective-permute-done((bf16[48,512]{1,0:T(8,128)(2,1)S(1)}, bf16[48,512]{1,0:T(8,128)(2,1)S(1)}, u32[]{:S(2)}, u32[]{:S(2)}) %collective-permute-start.2) | collective-permute-done | bytes 49184 | tf_op jit(solution)/shard_map/ppermute | solution.py:379
  80.1 1.3 %collective-permute-done.1.side_ref = bf16[48,512]{1,0:T(8,128)(2,1)S(1)} collective-permute-done((bf16[48,512]{1,0:T(8,128)(2,1)S(1)}, bf16[48,512]{1,0:T(8,128)(2,1)S(1)}, u32[]{:S(2)}, u32[]{:S(2)}) %collective-permute-start.1) | collective-permute-done | bytes 49184 | tf_op jit(solution)/shard_map/ppermute | solution.py:378
  81.5 0.0 collective-permute-done.core_ref
  81.5 6.3 %all-to-all-done.4.front_ref = bf16[64,8,128]{2,1,0:T(8,128)(2,1)S(1)} async-done(((bf16[64,8,128]{2,1,0:T(8,128)(2,1)}), bf16[64,8,128]{2,1,0:T(8,128)(2,1)S(1)}, u32[]{:S(2)}, u32[]{:S(2)}) %all-to-all-start.4) | async-done | bytes 131104 | tf_op jit(solution)/shard_map/all_to_all | solution.py:380
  87.8 0.7 last.1
  (2 shorter events, 0.0 us)
Async XLA Ops:
  0.6 9.9 %copy-start.4 = (s32[1024]{0:T(1024)S(1)}, s32[1024]{0:T(1024)}, u32[]{:S(2)}) copy-start(s32[1024]{0:T(1024)} %param.14) | copy-start | bytes 12292
  0.6 9.8 %copy-start = (s32[3,1024]{1,0:T(4,128)S(1)}, s32[3,1024]{1,0:T(4,128)}, u32[]{:S(2)}) copy-start(s32[3,1024]{1,0:T(4,128)} %connect_ref.3) | copy-start | bytes 36868
  0.7 9.8 %copy-start.1 = (bf16[3,512]{1,0:T(4,128)(2,1)S(1)}, bf16[3,512]{1,0:T(4,128)(2,1)}, u32[]{:S(2)}) copy-start(bf16[3,512]{1,0:T(4,128)(2,1)} %coords_ref.3) | copy-start | bytes 9220
  13.4 43.3 %copy-start.2 = (f32[1024]{0:T(1024)S(1)}, f32[1024]{0:T(1024)}, u32[]{:S(2)}) copy-start(f32[1024]{0:T(1024)} %param.11) | copy-start | bytes 12292
  13.4 43.3 %copy-start.3 = (s32[4,4]{1,0:T(4,128)S(1)}, s32[4,4]{1,0:T(4,128)}, u32[]{:S(2)}) copy-start(s32[4,4]{1,0:T(4,128)} %class_ref.1) | copy-start | bytes 196
  71.8 16.0 %all-to-all-start.4 = ((bf16[64,8,128]{2,1,0:T(8,128)(2,1)}), bf16[64,8,128]{2,1,0:T(8,128)(2,1)S(1)}, u32[]{:S(2)}, u32[]{:S(2)}) async-start(bf16[64,8,128]{2,1,0:T(8,128)(2,1)} %get-tuple-element.40), calls=%async_computation.4 | async-start | bytes 262144 | tf_op jit(solution)/shard_map/all_to_all | solution.py:380
  76.3 3.8 %collective-permute-start.2 = (bf16[48,512]{1,0:T(8,128)(2,1)S(1)}, bf16[48,512]{1,0:T(8,128)(2,1)S(1)}, u32[]{:S(2)}, u32[]{:S(2)}) collective-permute-start(bf16[48,512]{1,0:T(8,128)(2,1)S(1)} %get-tuple-element.41.own_ref), channel_id=1, source_target_pairs={{0,192},{64,128},{128,64},{192,0},{1,193},{65,129},{129,65},{193,1... | collective-permute-start | bytes 147464 | tf_op jit(solution)/shard_map/ppermute | solution.py:379
  76.4 5.0 %collective-permute-start.1 = (bf16[48,512]{1,0:T(8,128)(2,1)S(1)}, bf16[48,512]{1,0:T(8,128)(2,1)S(1)}, u32[]{:S(2)}, u32[]{:S(2)}) collective-permute-start(bf16[48,512]{1,0:T(8,128)(2,1)S(1)} %get-tuple-element.41.own_ref), channel_id=1, source_target_pairs={{0,128},{64,192},{128,0},{192,64},{1,129},{65,193},{129,1},{193,65... | collective-permute-start | bytes 147464 | tf_op jit(solution)/shard_map/ppermute | solution.py:378
  77.1 4.3 %collective-permute-start = (bf16[48,512]{1,0:T(8,128)(2,1)S(1)}, bf16[48,512]{1,0:T(8,128)(2,1)S(1)}, u32[]{:S(2)}, u32[]{:S(2)}) collective-permute-start(bf16[48,512]{1,0:T(8,128)(2,1)S(1)} %get-tuple-element.41.own_ref), channel_id=1, source_target_pairs={{0,64},{64,0},{128,192},{192,128},{1,65},{65,1},{129,193},{193,129... | collective-permute-start | bytes 147464 | tf_op jit(solution)/shard_map/ppermute | solution.py:377

commit v4 on v3

--- a/solution.py
+++ b/solution.py
@@ -23,9 +23,11 @@
     return jnp.where(mask, 1.0, 0.0).astype(BF)
 
 
-CAP = 48
+CAP = 40
+CAP_HALF = 24
 FAST = 1
-SLOTS = 192
+SLOTS = 176
+SLOT_HALF = 96
 
 
 def ranks(owner):
@@ -87,20 +89,20 @@
     chosen = one_hot(iota((CAP, 1024), 1) == chosen)
     picked = lax.dot_general(chosen, table, NT, preferred_element_type=F32)
     picked = jnp.concatenate([picked, jnp.zeros((CAP, 80), F32)], 1)
-    pool_ref[...] = jnp.broadcast_to(fold(picked, CAP).astype(BF)[None], pool_ref.shape)
-
-
-def fold(rows, count):
+    pool_ref[...] = jnp.broadcast_to(fold(picked, CAP, CAP_HALF).astype(BF)[None], pool_ref.shape)
+
+
+def fold(rows, count, half):
     third = rows[:, 256:384]
-    third = third[: count // 2] + pltpu.roll(third[count // 2 :], 64, 1)
-    return jnp.concatenate([rows[:, 0:128], rows[:, 128:256], third], 0)
-
-
-def unfold(pool, groups, count):
-    half = count // 2
+    turned = pltpu.roll(third[half:], 64, 1)
+    turned = jnp.concatenate([turned, jnp.zeros((2 * half - count, 128), F32)], 0)
+    return jnp.concatenate([rows[:, 0:128], rows[:, 128:256], third[:half] + turned], 0)
+
+
+def unfold(pool, groups, count, half):
     third = pool[:, 2 * count :, :]
     turned = pltpu.roll(third.reshape(groups * half, 128), 64, 1).reshape(groups, half, 128)
-    third = jnp.concatenate([third, turned], 1)
+    third = jnp.concatenate([third, turned[:, : count - half]], 1)
     blocks = [pool[:, 0:count, :], pool[:, count : 2 * count, :], third]
     return jnp.concatenate([block.reshape(groups * count, 128) for block in blocks], 1)
 
@@ -110,10 +112,25 @@
     outer = place_ref[1:2, :] - mine
     chosen = take(outer, SLOTS, place_ref[0:1, :].astype(F32)).astype(jnp.int32)
     chosen = one_hot(iota((SLOTS, 8 * CAP), 1) == chosen)
-    rows = unfold(pool_ref[...].astype(F32), 8, CAP).astype(BF)
+    rows = unfold(pool_ref[...].astype(F32), 8, CAP, CAP_HALF).astype(BF)
     rows = jnp.dot(chosen, rows, preferred_element_type=F32)
     rows = jnp.where(iota((SLOTS, 384), 1) < 320, rows, 0.0)
-    out_ref[...] = jnp.broadcast_to(fold(rows, SLOTS).astype(BF)[None], out_ref.shape)
+    out_ref[...] = jnp.broadcast_to(fold(rows, SLOTS, SLOT_HALF).astype(BF)[None], out_ref.shape)
+
+
+def join_kernel(state_ref, adjoint_ref, list_ref, out_ref, left_ref, right_ref, row_ref, sems):
+    copies = [
+        pltpu.make_async_copy(state_ref, left_ref, sems.at[0]),
+        pltpu.make_async_copy(adjoint_ref, right_ref, sems.at[1]),
+        pltpu.make_async_copy(list_ref, row_ref, sems.at[2]),
+    ]
+    for copy in copies:
+        copy.start()
+    for copy in copies:
+        copy.wait()
+    owner = (row_ref[...] >> 8).astype(F32)
+    pieces = [left_ref[...].astype(F32), right_ref[...].astype(F32), owner, jnp.zeros((7, 1024), F32)]
+    out_ref[...] = jnp.concatenate(pieces, 0).astype(BF)
 
 
 def whole_kernel(col_ref, table_ref, list_ref, rows_ref):
@@ -149,77 +166,84 @@
     nsum_ref,
     nhalf_ref,
     elem_ref,
+    place_ref,
 ):
     scale = (4096 * 65536) ** (-0.25) / 3.0
     weight = area_ref[...] * scale
-    pool = unfold(pool_ref[...], 8, SLOTS)
+    pool = jnp.transpose(unfold(pool_ref[...], 8, SLOTS, SLOT_HALF))[:304]
     chosen = one_hot(iota((8 * SLOTS, 1024), 0) == slot_ref[1:2, :])
-    found = lax.dot_general(pool, chosen, TN, preferred_element_type=F32)
+    found = jnp.dot(pool, chosen, preferred_element_type=F32)
     fpack_ref[...] = found[:288].astype(BF)
-    tail = jnp.transpose(found[256:384])
+    tail = found[288:304]
+    tail = [(tail[k : k + 1] + tail[3 + k : 4 + k] + tail[6 + k : 7 + k]) / 3.0 for k in range(3)]
+    tail = jnp.transpose(jnp.concatenate(tail + [jnp.zeros((5, 1024), F32)], 0))
     for k in range(3):
-        value = (tail[:, 32 + k : 33 + k] + tail[:, 35 + k : 36 + k] + tail[:, 38 + k : 39 + k]) / 3.0
-        frontx_ref[k] = jnp.broadcast_to(value, (1024, 128))
+        frontx_ref[k] = jnp.broadcast_to(tail[:, k : k + 1], (1024, 128))
     rows = [[points_ref[3 * a + k : 3 * a + k + 1, :] for k in range(3)] for a in range(3)]
     center = [(rows[0][k] + rows[1][k] + rows[2][k]) / 3.0 for k in range(3)]
     corner = [coords_ref[k : k + 1, :].astype(F32) for k in range(3)]
 
-    def fill(out_ref, place, first, count, lanes):
-        width = place[0].shape[1]
-        place = [jnp.broadcast_to(p, (16, width)) for p in place]
-
-        def chunk(step, carry):
-            at = pl.ds(pl.multiple_of(first + 16 * step, 16), 16)
-            offset = []
-            for k in range(3):
-                piece = frontx_ref[k, at, :]
-                offset.append(jnp.concatenate([piece] * (width // 128), 1) - place[k])
-            squared = offset[0] * offset[0] + offset[1] * offset[1] + offset[2] * offset[2] + SOFTEN
-            inverse = lax.rsqrt(squared)
-            factor = inverse * inverse * inverse
-            for k in range(3):
-                out_ref[k, at, lanes] = (offset[k] * factor).astype(BF)
-            return carry
-
-        lax.fori_loop(0, count // 16, chunk, 0, unroll=4)
-
-    for half in range(2):
-        lanes = slice(256 * half, 256 * half + 256)
-        fill(knode_ref, [c[:, lanes] for c in corner], 0, 1024, lanes)
-    for jt in range(4):
-        lanes = slice(256 * jt, 256 * jt + 256)
-        place = [c[:, lanes] for c in center]
-        for it in range(4):
-            vertex = class_ref[it, jt] == 1
-
-            @pl.when(vertex)
-            def _():
-                kcell_ref[:, 256 * it : 256 * it + 256, lanes] = jnp.zeros((3, 256, 256), BF)
-
-            @pl.when(jnp.logical_not(vertex))
-            def _():
-                fill(kcell_ref, place, 256 * it, 256, lanes)
+    mask = [[class_ref[it, jt].astype(F32) for jt in range(4)] for it in range(4)]
+
+    for k in range(3):
+        place_ref[k, :, 0:512] = jnp.broadcast_to(corner[k], (8, 512))
+        place_ref[k, :, 512:1536] = jnp.broadcast_to(center[k], (8, 1024))
+
+    def fill(out_ref, step, lanes, shift, soften):
+        at = slice(16 * step, 16 * step + 16)
+        offset = []
+        for k in range(3):
+            piece = frontx_ref[k, at, :]
+            place = place_ref[k, :, lanes.start + shift : lanes.stop + shift]
+            place = jnp.concatenate([place, place], 0)
+            offset.append(jnp.concatenate([piece, piece], 1) - place)
+        squared = offset[0] * offset[0] + offset[1] * offset[1] + offset[2] * offset[2] + soften
+        inverse = lax.rsqrt(squared)
+        factor = inverse * inverse * inverse
+        for k in range(3):
+            out_ref[k, at, lanes] = (offset[k] * factor).astype(BF)
+
+    def weave(many, few):
+        done = 0
+        for place, job in enumerate(many):
+            while done < len(few) and done * len(many) <= place * len(few):
+                few[done]()
+                done += 1
+            job()
+        for job in few[done:]:
+            job()
 
     share_ref[...] = (pack_ref[...].astype(F32) * weight).astype(BF)
     ends = [jnp.broadcast_to(connect_ref[a : a + 1, :] - col_ref[0] * 512, (16, 1024)) for a in range(3)]
 
-    def mark(step, carry):
-        at = pl.multiple_of(16 * step, 16)
-        node = iota((16, 1024), 0) + at
+    def mark(step):
+        node = iota((16, 1024), 0) + 16 * step
         hit = (node == ends[0]) | (node == ends[1]) | (node == ends[2])
-        touch_ref[pl.ds(at, 16), :] = one_hot(hit)
-        return carry
-
-    lax.fori_loop(0, 32, mark, 0, unroll=2)
-    for jt in range(4):
+        touch_ref[16 * step : 16 * step + 16, :] = one_hot(hit)
+
+    for step in range(32):
+        mark(step)
+
+    def part(jt):
         lanes = slice(256 * jt, 256 * jt + 256)
         part_ref[jt] = lax.dot_general(
             share_ref[:, lanes], touch_ref[:, lanes], NT, preferred_element_type=F32
         )
-    mask = [[class_ref[it, jt].astype(F32) for jt in range(4)] for it in range(4)]
-
-    def blend(step, carry):
-        at = pl.ds(pl.multiple_of(16 * step, 16), 16)
+
+    def node_fill(step, half):
+        fill(knode_ref, step, slice(256 * half, 256 * half + 256), 0, SOFTEN)
+
+    def cell_fill(step, jt):
+        soften = jnp.where(class_ref[step // 16, jt] == 1, 3.0e38, SOFTEN).astype(F32)
+        fill(kcell_ref, step, slice(256 * jt, 256 * jt + 256), 512, soften)
+
+    weave(
+        [lambda s=s, h=h: node_fill(s, h) for h in range(2) for s in range(64)],
+        [lambda jt=jt: part(jt) for jt in range(4)],
+    )
+
+    def blend(step):
+        at = slice(16 * step, 16 * step + 16)
         part = [part_ref[jt, at, :] for jt in range(4)]
         for it in range(4):
             total = part[0] * mask[it][0]
@@ -227,48 +251,60 @@
                 total = total + part[jt] * mask[it][jt]
             nsum_ref[it, at, :] = total
             nhalf_ref[it, at, :] = total.astype(BF)
-        return carry
-
-    lax.fori_loop(0, 18, blend, 0)
-
-    for jt in range(4):
+
+    nodes = [[], [], []]
+
+    def node_dot(k, it):
+        rows = slice(256 * it, 256 * it + 256)
+        product = jnp.dot(fpack_ref[:, rows], knode_ref[k, rows, :], preferred_element_type=F32)
+        nodes[k].append(load_sum(product * nsum_ref[it], 512))
+
+    def cell_dot(k, jt):
         lanes = slice(256 * jt, 256 * jt + 256)
         leader = pack_ref[:, lanes].astype(F32) * weight[:, lanes]
+        product = jnp.dot(fpack_ref[...], kcell_ref[k, :, lanes], preferred_element_type=F32)
+        elem_ref[16 * k : 16 * k + 16, lanes] = load_sum(product * leader, 256)
+
+    weave(
+        [lambda s=s, jt=jt: cell_fill(s, jt) for jt in range(2) for s in range(64)],
+        [lambda s=s: blend(s) for s in range(18)]
+        + [lambda k=k, it=it: node_dot(k, it) for k in range(3) for it in range(4)]
+        + [lambda k=k: cell_dot(k, 0) for k in range(3)],
+    )
+
+    pieces = [[] for it in range(4)]
+
+    def row_dot(k, it):
+        rows = slice(256 * it, 256 * it + 256)
+        product = 3.0 * lax.dot_general(
+            share_ref[...], kcell_ref[k, rows, :], NT, preferred_element_type=F32
+        ) + lax.dot_general(nhalf_ref[it], knode_ref[k, rows, :], NT, preferred_element_type=F32)
+        pieces[it].append(-load_sum(product * fpack_ref[:, rows].astype(F32), 256))
+
+    for it in range(4):
+        if it == 0:
+            few = [lambda k=k: cell_dot(k, 1) for k in range(3)]
+        else:
+            few = [lambda k=k, it=it: row_dot(k, it - 1) for k in range(3)]
+        weave([lambda s=s, jt=jt, it=it: cell_fill(16 * it + s, jt) for s in range(16) for jt in (2, 3)], few)
+    for k in range(3):
+        row_dot(k, 3)
+    for jt in (2, 3):
         for k in range(3):
-            product = jnp.dot(fpack_ref[...], kcell_ref[k, :, lanes], preferred_element_type=F32)
-            elem_ref[16 * k : 16 * k + 16, lanes] = load_sum(product * leader, 256)
-
-    nodes = []
-    for k in range(3):
-        total = None
-        for it in range(4):
-            rows = slice(256 * it, 256 * it + 256)
-            product = jnp.dot(fpack_ref[:, rows], knode_ref[k, rows, :], preferred_element_type=F32)
-            value = load_sum(product * nsum_ref[it], 512)
-            total = value if it == 0 else total + value
-        nodes.append(total)
+            cell_dot(k, jt)
+    nodes = jnp.concatenate([part[0] + part[1] + part[2] + part[3] for part in nodes], 0)
     value = elem_ref[...]
     high = value.astype(BF)
     low = (value - high.astype(F32)).astype(BF)
     spread = lax.dot_general(
         jnp.concatenate([high, low], 0), touch_ref[...], NT, preferred_element_type=F32
     )
-    node_ref[...] = (jnp.concatenate(nodes, 0) + (spread[:48] + spread[48:])).astype(BF)
+    node_ref[...] = (nodes + (spread[:48] + spread[48:])).astype(BF)
 
     columns = []
     for it in range(4):
-        rows = slice(256 * it, 256 * it + 256)
-        leader = fpack_ref[:, rows].astype(F32)
-        pieces = []
-        for k in range(3):
-            product = 3.0 * lax.dot_general(
-                share_ref[...], kcell_ref[k, rows, :], NT, preferred_element_type=F32
-            ) + lax.dot_general(
-                nhalf_ref[it], knode_ref[k, rows, :], NT, preferred_element_type=F32
-            )
-            pieces.append(-load_sum(product * leader, 256))
-        pieces.append(jnp.zeros((80, 256), F32))
-        columns.append(jnp.transpose(jnp.concatenate(pieces, 0)))
+        filled = jnp.concatenate(pieces[it] + [jnp.zeros((80, 256), F32)], 0)
+        columns.append(jnp.transpose(filled))
     turned = jnp.concatenate(columns, 0).reshape(64, 16, 128)
     packed = turned[:, :8] + pltpu.roll(turned[:, 8:].reshape(512, 128), 64, 1).reshape(64, 8, 128)
     front_ref[...] = packed.astype(BF)
@@ -288,22 +324,34 @@
 
 
 VMEM = pl.BlockSpec(memory_space=pltpu.VMEM)
+HBM = pl.BlockSpec(memory_space=pltpu.HBM)
 SMEM = pl.BlockSpec(memory_space=pltpu.SMEM)
 
 
 def body(state, adjoint, area, node_coords, connect, front_list, tile_class):
     col = lax.axis_index(COL).astype(jnp.int32).reshape(1)
-    owners = (front_list >> 8).astype(BF).reshape(1, 1024)
-    mine = jnp.concatenate([state.T, adjoint.T, owners, jnp.zeros((7, 1024), BF)], 0)
+    front_list = front_list.reshape(1, 1024)
+    mine = pl.pallas_call(
+        join_kernel,
+        out_shape=shape((80, 1024), BF),
+        in_specs=[HBM] * 3,
+        out_specs=VMEM,
+        scratch_shapes=[
+            pltpu.VMEM((36, 1024), BF),
+            pltpu.VMEM((36, 1024), BF),
+            pltpu.VMEM((1, 1024), jnp.int32),
+            pltpu.SemaphoreType.DMA((3,)),
+        ],
+        name="join",
+    )(state.T, adjoint.T, front_list)
     gathered = lax.all_gather(mine, ROW)
-    front_list = front_list.reshape(1, 1024)
     pack, points, table, pool, place, fits = pl.pallas_call(
         prep_kernel,
         out_shape=(
             shape((288, 1024), BF),
             shape((16, 1024), F32),
             shape((304, 1024), BF),
-            shape((8, CAP * 5 // 2, 128), BF),
+            shape((8, 2 * CAP + CAP_HALF, 128), BF),
             shape((2, 1024), jnp.int32),
             shape((1, 1), jnp.int32),
         ),
@@ -317,7 +365,7 @@
         part = lax.all_to_all(pool, "z", 0, 0)
         merged = pl.pallas_call(
             merge_kernel,
-            out_shape=shape((8, SLOTS * 5 // 2, 128), BF),
+            out_shape=shape((8, 2 * SLOTS + SLOT_HALF, 128), BF),
             in_specs=[SMEM] + [VMEM] * 2,
             out_specs=VMEM,
             compiler_params=pltpu.CompilerParams(vmem_limit_bytes=24 << 20),
@@ -338,8 +386,8 @@
         spread = jnp.broadcast_to(share[None], (64, 16, 384))
         rows = lax.all_to_all(spread, COL, 0, 0).reshape(1024, 384)
         rows = jnp.pad(rows, ((0, 8 * SLOTS - 1024), (0, 0))).reshape(8, SLOTS, 384)
-        third = rows[:, :, 256:320].reshape(8, 2, SLOTS // 2, 64)
-        third = jnp.concatenate([third[:, 0], third[:, 1]], 2)
+        third = jnp.pad(rows[:, :, 256:320], ((0, 0), (0, 2 * SLOT_HALF - SLOTS), (0, 0)))
+        third = jnp.concatenate([third[:, :SLOT_HALF], third[:, SLOT_HALF:]], 2)
         pool = jnp.concatenate([rows[:, :, 0:128], rows[:, :, 128:256], third], 1)
         return pool, jnp.broadcast_to(jnp.arange(1024, dtype=jnp.int32), (2, 1024))
 
@@ -360,6 +408,7 @@
             pltpu.VMEM((4, 288, 512), F32),
             pltpu.VMEM((4, 288, 512), BF),
             pltpu.VMEM((48, 1024), F32),
+            pltpu.VMEM((3, 8, 1536), F32),
         ],
         compiler_params=pltpu.CompilerParams(vmem_limit_bytes=44 << 20),
         name="sweep",

time: 89.2 us -> 83.9 us (0.941)
  blocking collectives: 50.7 us -> 48.6 us
  other arithmetic: 1.75 us -> 0 us
  Pallas kernels: 18.6 us -> 16.9 us
    pallas_call x1, Pallas kernels: 15.1 us -> 11.8 us  [body(): pl.pallas_call(main_kernel, out_shape=(shape((64, 8, 128), BF), shape((48...]
    ppermute x1, waiting for transfers between devices: 1.31 us -> 3.25 us  [body(): side = lax.ppermute(node_part, ROW, [(i, i ^ 2) for i in range(4)])]
    ppermute x1, waiting for transfers between devices: 1.85 us -> 0.08 us  [body(): cross = lax.ppermute(node_part, ROW, [(i, i ^ 3) for i in range(4)])]
    all_to_all x1, blocking collectives: 22.4 us -> 20.8 us  [compact(): return (lax.all_to_all(merged, ('yh', 'x'), 0, 0), place)]
    pallas_call x1 -> x2, Pallas kernels: 0.49 us -> 2.07 us  [the longest x1 1.66 us: body(): pl.pallas_call(join_kernel, out_shape=shape((80, 1024), BF), in_specs=[HB...]
    ppermute x1, starting transfers between devices: 0.09 us -> 1.29 us  [body(): cross = lax.ppermute(node_part, ROW, [(i, i ^ 3) for i in range(4)])]
    ppermute x1, starting transfers between devices: 1.18 us -> 0.09 us  [body(): core = lax.ppermute(node_part, ROW, [(i, i ^ 1) for i in range(4)])]
    concatenate x1 -> x0, other arithmetic: 1.02 us -> none  [body(): jnp.concatenate([state.T, adjoint.T, owners, jnp.zeros((7, 1024), BF)], 0)]
where the time goes in v4:
time: 83.9 us; the launch traced here: 83.7 us
  blocking collectives  48.6 us (58%)
  Pallas kernels  16.9 us (20%)
  waiting for transfers between devices  9.45 us (11%)
  starting transfers between devices  7.32 us (9%)
  between operations  1.37 us (2%)
    all_to_all x1, blocking collectives, compact(): return (lax.all_to_all(merged, ('yh', 'x'), 0, 0), place)  20.8 us
    all_to_all x1, blocking collectives, compact(): part = lax.all_to_all(pool, 'z', 0, 0)  19.6 us
    pallas_call x1, Pallas kernels, body(): pl.pallas_call(main_kernel, out_shape=(shape((64, 8, 128), BF), shape((48...  11.8 us
    all_gather x1, blocking collectives, body(): gathered = lax.all_gather(mine, ROW)  8.18 us
    all_to_all x1, waiting for transfers between devices, body(): front_sum = lax.all_to_all(front_part, COL, 0, 0)  6.12 us
    all_to_all x1, starting transfers between devices, body(): front_sum = lax.all_to_all(front_part, COL, 0, 0)  5.38 us
    ppermute x1, waiting for transfers between devices, body(): side = lax.ppermute(node_part, ROW, [(i, i ^ 2) for i in range(4)])  3.25 us
    pallas_call x1, Pallas kernels, body(): pl.pallas_call(prep_kernel, out_shape=(shape((288, 1024), BF), shape((16,...  2.27 us
  transfers between devices with their start and end apart: 4, of which 3 were waited for; matrix products, arithmetic and copies ran while one was open for 0% of the time, Pallas kernels for 0%

profile of v4, /device:TPU:2, one launch (start us, length us, event | category | flops | bytes accessed | tf_op | source)
XLA Modules:
  0.0 83.7 jit_solution(16091080547894307912)
XLA Ops:
  0.6 0.0 copy-start.4
  0.6 0.0 copy-start
  0.7 0.0 copy-start.1
  0.7 1.7 %join.1 = bf16[80,1024]{1,0:T(8,128)(2,1)} custom-call(bf16[36,1024]{1,0:T(8,128)(2,1)} %bitcast.18, bf16[36,1024]{1,0:T(8,128)(2,1)} %bitcast.19, s32[1,1024]{1,0:T(1,128)} %bitcast.20), custom_call_target="tpu_custom_call" | custom-call | tf_op jit(solution)/shard_map/join/pallas_call | solution.py:334
  2.3 8.2 %all-gather = bf16[320,1024]{1,0:T(8,128)(2,1)S(1)} all-gather(bf16[80,1024]{1,0:T(8,128)(2,1)} %join.1), channel_id=2, replica_groups=mesh['yl'=2,'co'=2,'z'=8,'yh'=2,'x'=4] {'yl','co'}, dimensions={0}, use_global_device_ids=true | all-gather | bytes 819200 | tf_op jit(solution)/shard_map/all_gather | solution.py:347
  10.5 0.0 copy-done.4
  10.5 0.0 copy-done
  10.5 0.0 copy-done.1
  10.5 2.3 %prep.1 = (bf16[288,1024]{1,0:T(8,128)(2,1)S(1)}, f32[16,1024]{1,0:T(8,128)S(1)}, bf16[304,1024]{1,0:T(8,128)(2,1)S(1)}, bf16[8,104,128]{2,1,0:T(8,128)(2,1)S(1)...) custom-call(s32[1]{0:T(128)} %bitcast.3.col_ref, bf16[4,80,1024]{2,1,0:T(8,128)(2,1)S(1)} %bitcast.11, s32[3,1024]{1,0:T(4,128)S(1)} %copy-done, ...), custom_call_target="tpu_custom_call" | custom-call | tf_op jit(solution)/shard_map/prep/pallas_call | solution.py:348
  13.4 0.0 copy-start.2
  13.5 0.0 copy-start.3
  13.5 40.9 %conditional.1 = (bf16[8,448,128]{2,1,0:T(8,128)(2,1)S(1)}, s32[2,1024]{1,0:T(2,128)S(1)}) conditional(s32[]{:T(128)} %bitcast.9, (s32[1]{0:T(128)}, bf16[304,1024]{1,0:T(8,128)(2,1)S(1)}, s32[1,1024]{1,0:T(1,128)S(1)}) %tuple.22, (bf16[8,104,128]{2,1,0:T(8,128)(2,1)S(1)}, s32[1]{0:T(128)}, s32[2,1024]{1,0:T(2,128)S(1)}) %tuple.17), branch_computations={%region_0.2_spmd, %region_2.3_spmd} | conditional | flops 4057088 | bytes 10731540 | solution.py:394
  13.5 19.6 %all_to_all.23.pool_ref = bf16[8,104,128]{2,1,0:T(8,128)(2,1)S(1)} all-to-all(bf16[8,104,128]{2,1,0:T(8,128)(2,1)S(1)} %get-tuple-element.16), channel_id=1, replica_groups=mesh['yl'=2,'co'=2,'z'=8,'yh'=2,'x'=4] {'z'}, dimensions={0} | all-to-all | bytes 425984 | tf_op jit(solution)/shard_map/cond/branch_1_fun/all_to_all | solution.py:365
  33.1 0.4 merge.1
  33.5 20.8 %all_to_all.24 = bf16[8,448,128]{2,1,0:T(8,128)(2,1)S(1)} all-to-all(bf16[8,448,128]{2,1,0:T(8,128)(2,1)S(1)} %merge.1), channel_id=1, replica_groups=mesh['yl'=2,'co'=2,'z'=8,'yh'=2,'x'=4] {'yh','x'}, dimensions={0} | all-to-all | bytes 1835008 | tf_op jit(solution)/shard_map/cond/branch_1_fun/all_to_all | solution.py:374
  54.3 0.0 copy-done.2
  54.3 0.0 copy-done.3
  54.3 11.8 %sweep.1 = (bf16[64,8,128]{2,1,0:T(8,128)(2,1)}, bf16[48,512]{1,0:T(8,128)(2,1)S(1)}) custom-call(s32[1]{0:T(128)} %bitcast.3.col_ref, s32[4,4]{1,0:T(4,128)S(1)} %copy-done.3, bf16[288,1024]{1,0:T(8,128)(2,1)S(1)} %get-tuple-element.32.pack_ref, f32[16,1024]{1,0:T(8,128)S(1)} %get-tuple-element.33.points_ref, f32[1,1024]{1,0:T(1,128)S(1)} %bitcast.12, ...), custom_call_target="tpu_custom_call" | custom-call | tf_op jit(solution)/shard_map/sweep/pallas_call | solution.py:395
  66.1 5.4 %all-to-all-start.4 = ((bf16[64,8,128]{2,1,0:T(8,128)(2,1)}), bf16[64,8,128]{2,1,0:T(8,128)(2,1)S(1)}, u32[]{:S(2)}, u32[]{:S(2)}) async-start(bf16[64,8,128]{2,1,0:T(8,128)(2,1)} %get-tuple-element.40), calls=%async_computation.4 | async-start | bytes 262144 | tf_op jit(solution)/shard_map/all_to_all | solution.py:429
  71.5 0.1 collective-permute-start
  71.6 0.6 collective-permute-start.1
  72.2 1.3 %collective-permute-start.2 = (bf16[48,512]{1,0:T(8,128)(2,1)S(1)}, bf16[48,512]{1,0:T(8,128)(2,1)S(1)}, u32[]{:S(2)}, u32[]{:S(2)}) collective-permute-start(bf16[48,512]{1,0:T(8,128)(2,1)S(1)} %get-tuple-element.41.own_ref), channel_id=1, source_target_pairs={{0,192},{64,128},{128,64},{192,0},{1,193},{65,129},{129,65},{193,1... | collective-permute-start | bytes 147464 | tf_op jit(solution)/shard_map/ppermute | solution.py:428
  73.5 0.0 collective-permute-done.core_ref
  73.5 3.2 %collective-permute-done.1.side_ref = bf16[48,512]{1,0:T(8,128)(2,1)S(1)} collective-permute-done((bf16[48,512]{1,0:T(8,128)(2,1)S(1)}, bf16[48,512]{1,0:T(8,128)(2,1)S(1)}, u32[]{:S(2)}, u32[]{:S(2)}) %collective-permute-start.1) | collective-permute-done | bytes 49184 | tf_op jit(solution)/shard_map/ppermute | solution.py:427
  76.7 0.1 collective-permute-done.2.cross_ref
  76.8 6.1 %all-to-all-done.4.front_ref = bf16[64,8,128]{2,1,0:T(8,128)(2,1)S(1)} async-done(((bf16[64,8,128]{2,1,0:T(8,128)(2,1)}), bf16[64,8,128]{2,1,0:T(8,128)(2,1)S(1)}, u32[]{:S(2)}, u32[]{:S(2)}) %all-to-all-start.4) | async-done | bytes 131104 | tf_op jit(solution)/shard_map/all_to_all | solution.py:429
  82.9 0.7 last.1
Async XLA Ops:
  0.6 9.9 %copy-start.4 = (s32[1024]{0:T(1024)S(1)}, s32[1024]{0:T(1024)}, u32[]{:S(2)}) copy-start(s32[1024]{0:T(1024)} %param.14) | copy-start | bytes 12292
  0.6 9.9 %copy-start = (s32[3,1024]{1,0:T(4,128)S(1)}, s32[3,1024]{1,0:T(4,128)}, u32[]{:S(2)}) copy-start(s32[3,1024]{1,0:T(4,128)} %connect_ref.3) | copy-start | bytes 36868
  0.7 9.9 %copy-start.1 = (bf16[3,512]{1,0:T(4,128)(2,1)S(1)}, bf16[3,512]{1,0:T(4,128)(2,1)}, u32[]{:S(2)}) copy-start(bf16[3,512]{1,0:T(4,128)(2,1)} %coords_ref.3) | copy-start | bytes 9220
  13.4 40.9 %copy-start.2 = (f32[1024]{0:T(1024)S(1)}, f32[1024]{0:T(1024)}, u32[]{:S(2)}) copy-start(f32[1024]{0:T(1024)} %param.11) | copy-start | bytes 12292
  13.5 40.9 %copy-start.3 = (s32[4,4]{1,0:T(4,128)S(1)}, s32[4,4]{1,0:T(4,128)}, u32[]{:S(2)}) copy-start(s32[4,4]{1,0:T(4,128)} %class_ref.1) | copy-start | bytes 196
  66.1 16.8 %all-to-all-start.4 = ((bf16[64,8,128]{2,1,0:T(8,128)(2,1)}), bf16[64,8,128]{2,1,0:T(8,128)(2,1)S(1)}, u32[]{:S(2)}, u32[]{:S(2)}) async-start(bf16[64,8,128]{2,1,0:T(8,128)(2,1)} %get-tuple-element.40), calls=%async_computation.4 | async-start | bytes 262144 | tf_op jit(solution)/shard_map/all_to_all | solution.py:429
  71.5 2.0 %collective-permute-start = (bf16[48,512]{1,0:T(8,128)(2,1)S(1)}, bf16[48,512]{1,0:T(8,128)(2,1)S(1)}, u32[]{:S(2)}, u32[]{:S(2)}) collective-permute-start(bf16[48,512]{1,0:T(8,128)(2,1)S(1)} %get-tuple-element.41.own_ref), channel_id=1, source_target_pairs={{0,64},{64,0},{128,192},{192,128},{1,65},{65,1},{129,193},{193,129... | collective-permute-start | bytes 147464 | tf_op jit(solution)/shard_map/ppermute | solution.py:426
  71.6 5.1 %collective-permute-start.1 = (bf16[48,512]{1,0:T(8,128)(2,1)S(1)}, bf16[48,512]{1,0:T(8,128)(2,1)S(1)}, u32[]{:S(2)}, u32[]{:S(2)}) collective-permute-start(bf16[48,512]{1,0:T(8,128)(2,1)S(1)} %get-tuple-element.41.own_ref), channel_id=1, source_target_pairs={{0,128},{64,192},{128,0},{192,64},{1,129},{65,193},{129,1},{193,65... | collective-permute-start | bytes 147464 | tf_op jit(solution)/shard_map/ppermute | solution.py:427
  72.2 4.6 %collective-permute-start.2 = (bf16[48,512]{1,0:T(8,128)(2,1)S(1)}, bf16[48,512]{1,0:T(8,128)(2,1)S(1)}, u32[]{:S(2)}, u32[]{:S(2)}) collective-permute-start(bf16[48,512]{1,0:T(8,128)(2,1)S(1)} %get-tuple-element.41.own_ref), channel_id=1, source_target_pairs={{0,192},{64,128},{128,64},{192,0},{1,193},{65,129},{129,65},{193,1... | collective-permute-start | bytes 147464 | tf_op jit(solution)/shard_map/ppermute | solution.py:428

commit v5 on v4

--- a/solution.py
+++ b/solution.py
@@ -24,10 +24,10 @@
 
 
 CAP = 40
-CAP_HALF = 24
+CAP_PART = 16
 FAST = 1
 SLOTS = 176
-SLOT_HALF = 96
+SLOT_PART = 64
 
 
 def ranks(owner):
@@ -89,20 +89,25 @@
     chosen = one_hot(iota((CAP, 1024), 1) == chosen)
     picked = lax.dot_general(chosen, table, NT, preferred_element_type=F32)
     picked = jnp.concatenate([picked, jnp.zeros((CAP, 80), F32)], 1)
-    pool_ref[...] = jnp.broadcast_to(fold(picked, CAP, CAP_HALF).astype(BF)[None], pool_ref.shape)
-
-
-def fold(rows, count, half):
-    third = rows[:, 256:384]
-    turned = pltpu.roll(third[half:], 64, 1)
-    turned = jnp.concatenate([turned, jnp.zeros((2 * half - count, 128), F32)], 0)
-    return jnp.concatenate([rows[:, 0:128], rows[:, 128:256], third[:half] + turned], 0)
-
-
-def unfold(pool, groups, count, half):
-    third = pool[:, 2 * count :, :]
-    turned = pltpu.roll(third.reshape(groups * half, 128), 64, 1).reshape(groups, half, 128)
-    third = jnp.concatenate([third, turned[:, : count - half]], 1)
+    pool_ref[...] = jnp.broadcast_to(fold(picked, CAP, CAP_PART).astype(BF)[None], pool_ref.shape)
+
+
+def fold(rows, count, part):
+    third = jnp.concatenate([rows[:, 256:384], jnp.zeros((3 * part - count, 128), F32)], 0)
+    third = (
+        third[:part]
+        + pltpu.roll(third[part : 2 * part], 42, 1)
+        + pltpu.roll(third[2 * part :], 84, 1)
+    )
+    return jnp.concatenate([rows[:, 0:128], rows[:, 128:256], third], 0)
+
+
+def unfold(pool, groups, count, part):
+    first = pool[:, 2 * count :, :]
+    flat = first.reshape(groups * part, 128)
+    second = pltpu.roll(flat, 86, 1).reshape(groups, part, 128)
+    third = pltpu.roll(flat, 44, 1).reshape(groups, part, 128)
+    third = jnp.concatenate([first, second, third[:, : count - 2 * part]], 1)
     blocks = [pool[:, 0:count, :], pool[:, count : 2 * count, :], third]
     return jnp.concatenate([block.reshape(groups * count, 128) for block in blocks], 1)
 
@@ -112,25 +117,10 @@
     outer = place_ref[1:2, :] - mine
     chosen = take(outer, SLOTS, place_ref[0:1, :].astype(F32)).astype(jnp.int32)
     chosen = one_hot(iota((SLOTS, 8 * CAP), 1) == chosen)
-    rows = unfold(pool_ref[...].astype(F32), 8, CAP, CAP_HALF).astype(BF)
+    rows = unfold(pool_ref[...].astype(F32), 8, CAP, CAP_PART).astype(BF)
     rows = jnp.dot(chosen, rows, preferred_element_type=F32)
-    rows = jnp.where(iota((SLOTS, 384), 1) < 320, rows, 0.0)
-    out_ref[...] = jnp.broadcast_to(fold(rows, SLOTS, SLOT_HALF).astype(BF)[None], out_ref.shape)
-
-
-def join_kernel(state_ref, adjoint_ref, list_ref, out_ref, left_ref, right_ref, row_ref, sems):
-    copies = [
-        pltpu.make_async_copy(state_ref, left_ref, sems.at[0]),
-        pltpu.make_async_copy(adjoint_ref, right_ref, sems.at[1]),
-        pltpu.make_async_copy(list_ref, row_ref, sems.at[2]),
-    ]
-    for copy in copies:
-        copy.start()
-    for copy in copies:
-        copy.wait()
-    owner = (row_ref[...] >> 8).astype(F32)
-    pieces = [left_ref[...].astype(F32), right_ref[...].astype(F32), owner, jnp.zeros((7, 1024), F32)]
-    out_ref[...] = jnp.concatenate(pieces, 0).astype(BF)
+    rows = jnp.where(iota((SLOTS, 384), 1) < 298, rows, 0.0)
+    out_ref[...] = jnp.broadcast_to(fold(rows, SLOTS, SLOT_PART).astype(BF)[None], out_ref.shape)
 
 
 def whole_kernel(col_ref, table_ref, list_ref, rows_ref):
@@ -170,7 +160,18 @@
 ):
     scale = (4096 * 65536) ** (-0.25) / 3.0
     weight = area_ref[...] * scale
-    pool = jnp.transpose(unfold(pool_ref[...], 8, SLOTS, SLOT_HALF))[:304]
+    share_ref[...] = (pack_ref[...].astype(F32) * weight).astype(BF)
+    ends = [jnp.broadcast_to(connect_ref[a : a + 1, :] - col_ref[0] * 512, (16, 1024)) for a in range(3)]
+
+    def mark(step):
+        node = iota((16, 1024), 0) + 16 * step
+        hit = (node == ends[0]) | (node == ends[1]) | (node == ends[2])
+        touch_ref[16 * step : 16 * step + 16, :] = one_hot(hit)
+
+    for step in range(32):
+        mark(step)
+
+    pool = jnp.transpose(unfold(pool_ref[...], 8, SLOTS, SLOT_PART))[:304]
     chosen = one_hot(iota((8 * SLOTS, 1024), 0) == slot_ref[1:2, :])
     found = jnp.dot(pool, chosen, preferred_element_type=F32)
     fpack_ref[...] = found[:288].astype(BF)
@@ -212,17 +213,6 @@
             job()
         for job in few[done:]:
             job()
-
-    share_ref[...] = (pack_ref[...].astype(F32) * weight).astype(BF)
-    ends = [jnp.broadcast_to(connect_ref[a : a + 1, :] - col_ref[0] * 512, (16, 1024)) for a in range(3)]
-
-    def mark(step):
-        node = iota((16, 1024), 0) + 16 * step
-        hit = (node == ends[0]) | (node == ends[1]) | (node == ends[2])
-        touch_ref[16 * step : 16 * step + 16, :] = one_hot(hit)
-
-    for step in range(32):
-        mark(step)
 
     def part(jt):
         lanes = slice(256 * jt, 256 * jt + 256)
@@ -324,26 +314,14 @@
 
 
 VMEM = pl.BlockSpec(memory_space=pltpu.VMEM)
-HBM = pl.BlockSpec(memory_space=pltpu.HBM)
 SMEM = pl.BlockSpec(memory_space=pltpu.SMEM)
 
 
 def body(state, adjoint, area, node_coords, connect, front_list, tile_class):
     col = lax.axis_index(COL).astype(jnp.int32).reshape(1)
     front_list = front_list.reshape(1, 1024)
-    mine = pl.pallas_call(
-        join_kernel,
-        out_shape=shape((80, 1024), BF),
-        in_specs=[HBM] * 3,
-        out_specs=VMEM,
-        scratch_shapes=[
-            pltpu.VMEM((36, 1024), BF),
-            pltpu.VMEM((36, 1024), BF),
-            pltpu.VMEM((1, 1024), jnp.int32),
-            pltpu.SemaphoreType.DMA((3,)),
-        ],
-        name="join",
-    )(state.T, adjoint.T, front_list)
+    owners = (front_list >> 8).astype(BF)
+    mine = jnp.concatenate([state.T, adjoint.T, owners, jnp.zeros((7, 1024), BF)], 0)
     gathered = lax.all_gather(mine, ROW)
     pack, points, table, pool, place, fits = pl.pallas_call(
         prep_kernel,
@@ -351,7 +329,7 @@
             shape((288, 1024), BF),
             shape((16, 1024), F32),
             shape((304, 1024), BF),
-            shape((8, 2 * CAP + CAP_HALF, 128), BF),
+            shape((8, 2 * CAP + CAP_PART, 128), BF),
             shape((2, 1024), jnp.int32),
             shape((1, 1), jnp.int32),
         ),
@@ -365,7 +343,7 @@
         part = lax.all_to_all(pool, "z", 0, 0)
         merged = pl.pallas_call(
             merge_kernel,
-            out_shape=shape((8, 2 * SLOTS + SLOT_HALF, 128), BF),
+            out_shape=shape((8, 2 * SLOTS + SLOT_PART, 128), BF),
             in_specs=[SMEM] + [VMEM] * 2,
             out_specs=VMEM,
             compiler_params=pltpu.CompilerParams(vmem_limit_bytes=24 << 20),
@@ -386,8 +364,10 @@
         spread = jnp.broadcast_to(share[None], (64, 16, 384))
         rows = lax.all_to_all(spread, COL, 0, 0).reshape(1024, 384)
         rows = jnp.pad(rows, ((0, 8 * SLOTS - 1024), (0, 0))).reshape(8, SLOTS, 384)
-        third = jnp.pad(rows[:, :, 256:320], ((0, 0), (0, 2 * SLOT_HALF - SLOTS), (0, 0)))
-        third = jnp.concatenate([third[:, :SLOT_HALF], third[:, SLOT_HALF:]], 2)
+        third = jnp.pad(rows[:, :, 256:298], ((0, 0), (0, 3 * SLOT_PART - SLOTS), (0, 0)))
+        third = third.reshape(8, 3, SLOT_PART, 42)
+        third = jnp.concatenate([third[:, 0], third[:, 1], third[:, 2]], 2)
+        third = jnp.pad(third, ((0, 0), (0, 0), (0, 2)))
         pool = jnp.concatenate([rows[:, :, 0:128], rows[:, :, 128:256], third], 1)
         return pool, jnp.broadcast_to(jnp.arange(1024, dtype=jnp.int32), (2, 1024))
 

time: 83.9 us -> 83.1 us (level)
  other arithmetic: 0 us -> 1.75 us
  Pallas kernels: 16.9 us -> 15.4 us
  blocking collectives: 48.6 us -> 47.2 us
    pallas_call x2 -> x1, Pallas kernels: 2.07 us -> 0.42 us  [compact(): pl.pallas_call(merge_kernel, out_shape=shape((8, 2 * SLOTS + SLOT_PART, 1...]
    concatenate x0 -> x1, other arithmetic: none -> 1.02 us  [body(): jnp.concatenate([state.T, adjoint.T, owners, jnp.zeros((7, 1024), BF)], 0)]
    all_to_all x1, blocking collectives: 20.8 us -> 20 us  [compact(): return (lax.all_to_all(merged, ('yh', 'x'), 0, 0), place)]
where the time goes in v5:
time: 83.1 us; the launch traced here: 82.7 us
  blocking collectives  47.2 us (57%)
  Pallas kernels  15.4 us (19%)
  waiting for transfers between devices  9.45 us (11%)
  starting transfers between devices  7.48 us (9%)
  other arithmetic  1.75 us (2%)
  between operations  1.36 us (2%)
    all_to_all x1, blocking collectives, compact(): return (lax.all_to_all(merged, ('yh', 'x'), 0, 0), place)  20 us
    all_to_all x1, blocking collectives, compact(): part = lax.all_to_all(pool, 'z', 0, 0)  19.3 us
    pallas_call x1, Pallas kernels, body(): pl.pallas_call(main_kernel, out_shape=(shape((64, 8, 128), BF), shape((48...  11.9 us
    all_gather x1, blocking collectives, body(): gathered = lax.all_gather(mine, ROW)  7.97 us
    all_to_all x1, waiting for transfers between devices, body(): front_sum = lax.all_to_all(front_part, COL, 0, 0)  6.12 us
    all_to_all x1, starting transfers between devices, body(): front_sum = lax.all_to_all(front_part, COL, 0, 0)  5.54 us
    ppermute x1, waiting for transfers between devices, body(): side = lax.ppermute(node_part, ROW, [(i, i ^ 2) for i in range(4)])  3.25 us
    pallas_call x1, Pallas kernels, body(): pl.pallas_call(prep_kernel, out_shape=(shape((288, 1024), BF), shape((16,...  2.32 us
  transfers between devices with their start and end apart: 4, of which 3 were waited for; matrix products, arithmetic and copies ran while one was open for 0% of the time, Pallas kernels for 0%

profile of v5, /device:TPU:2, one launch (start us, length us, event | category | flops | bytes accessed | tf_op | source)
XLA Modules:
  0.0 82.7 jit_solution(1423249769284669810)
XLA Ops:
  0.6 0.0 copy-start.4
  0.6 0.0 copy-start
  0.7 0.0 copy-start.1
  0.7 0.7 shift-right-arithmetic_convert_fusion
  1.4 0.1 pad.21.clone
  1.5 1.0 %maximum_maximum_fusion = bf16[80,1024]{1,0:T(8,128)(2,1)S(1)} fusion(bf16[1,1024]{1,0:T(2,128)(2,1)S(1)} %convert_element_type.19, bf16[36,1024]{1,0:T(8,128)(2,1)} %bitcast.31, bf16[36,1024]{1,0:T(8,128)(2,1)} %bitcast.32, bf16[80]{0:T(256)(128)(2,1)S(1)} %pad.21.clone), kind=kLoop, calls=%fused_computation.10 | loop fusion | flops 655360 | bytes 313504 | tf_op jit(solution)/shard_map/concatenate | solution.py:324
  2.5 8.0 %all-gather = bf16[320,1024]{1,0:T(8,128)(2,1)S(1)} all-gather(bf16[80,1024]{1,0:T(8,128)(2,1)S(1)} %maximum_maximum_fusion), channel_id=2, replica_groups=mesh['yl'=2,'co'=2,'z'=8,'yh'=2,'x'=4] {'yl','co'}, dimensions={0}, use_global_device_ids=true | all-gather | bytes 819200 | tf_op jit(solution)/shard_map/all_gather | solution.py:325
  10.5 0.0 copy-done.4
  10.5 0.0 copy-done
  10.5 0.0 copy-done.1
  10.5 2.3 %prep.1 = (bf16[288,1024]{1,0:T(8,128)(2,1)S(1)}, f32[16,1024]{1,0:T(8,128)S(1)}, bf16[304,1024]{1,0:T(8,128)(2,1)S(1)}, bf16[8,96,128]{2,1,0:T(8,128)(2,1)S(1)}, s32[2,1024]{1,0:T(2,128)S(1)}, /*index=5*/s32[1,1]{1,0:T(1,128)}) custom-call(s32[1]{0:T(128)} %bitcast.7.col_ref, bf16[4,80,1024]{2,1,0:T(8,128)(2,1)S(1)} %bitcast.24, s32[3,1024]{1,0:T(4,128)S(1)} %copy-done, ...), custom_call_target="tpu_custom_call" | custom-call | tf_op jit(solution)/shard_map/prep/pallas_call | solution.py:326
  13.5 0.0 copy-start.2
  13.5 0.0 copy-start.3
  13.5 39.7 %conditional.1 = (bf16[8,416,128]{2,1,0:T(8,128)(2,1)S(1)}, s32[2,1024]{1,0:T(2,128)S(1)}) conditional(s32[]{:T(128)} %bitcast.13, (s32[1]{0:T(128)}, bf16[304,1024]{1,0:T(8,128)(2,1)S(1)}, s32[1,1024]{1,0:T(1,128)S(1)}) %tuple.25, (bf16[8,96,128]{2,1,0:T(8,128)(2,1)S(1)}, s32[1]{0:T(128)}, s32[2,1024]{1,0:T(2,128)S(1)}) %tuple.17), branch_computations={%region_0.2_spmd, %region_2.3_spmd} | conditional | flops 3598336 | bytes 10766870 | solution.py:374
  13.5 19.3 %all_to_all.23.pool_ref = bf16[8,96,128]{2,1,0:T(8,128)(2,1)S(1)} all-to-all(bf16[8,96,128]{2,1,0:T(8,128)(2,1)S(1)} %get-tuple-element.16), channel_id=1, replica_groups=mesh['yl'=2,'co'=2,'z'=8,'yh'=2,'x'=4] {'z'}, dimensions={0} | all-to-all | bytes 393216 | tf_op jit(solution)/shard_map/cond/branch_1_fun/all_to_all | solution.py:343
  32.8 0.4 merge.1
  33.2 20.0 %all_to_all.24 = bf16[8,416,128]{2,1,0:T(8,128)(2,1)S(1)} all-to-all(bf16[8,416,128]{2,1,0:T(8,128)(2,1)S(1)} %merge.1), channel_id=1, replica_groups=mesh['yl'=2,'co'=2,'z'=8,'yh'=2,'x'=4] {'yh','x'}, dimensions={0} | all-to-all | bytes 1703936 | tf_op jit(solution)/shard_map/cond/branch_1_fun/all_to_all | solution.py:352
  53.1 0.0 copy-done.2
  53.1 0.0 copy-done.3
  53.1 11.9 %sweep.1 = (bf16[64,8,128]{2,1,0:T(8,128)(2,1)}, bf16[48,512]{1,0:T(8,128)(2,1)S(1)}) custom-call(s32[1]{0:T(128)} %bitcast.7.col_ref, s32[4,4]{1,0:T(4,128)S(1)} %copy-done.3, bf16[288,1024]{1,0:T(8,128)(2,1)S(1)} %get-tuple-element.32.pack_ref, f32[16,1024]{1,0:T(8,128)S(1)} %get-tuple-element.33.points_ref, f32[1,1024]{1,0:T(1,128)S(1)} %bitcast.25, ...), custom_call_target="tpu_custom_call" | custom-call | tf_op jit(solution)/shard_map/sweep/pallas_call | solution.py:375
  65.1 5.5 %all-to-all-start.4 = ((bf16[64,8,128]{2,1,0:T(8,128)(2,1)}), bf16[64,8,128]{2,1,0:T(8,128)(2,1)S(1)}, u32[]{:S(2)}, u32[]{:S(2)}) async-start(bf16[64,8,128]{2,1,0:T(8,128)(2,1)} %get-tuple-element.40), calls=%async_computation.4 | async-start | bytes 262144 | tf_op jit(solution)/shard_map/all_to_all | solution.py:409
  70.6 0.1 collective-permute-start
  70.7 0.6 collective-permute-start.1
  71.3 1.3 %collective-permute-start.2 = (bf16[48,512]{1,0:T(8,128)(2,1)S(1)}, bf16[48,512]{1,0:T(8,128)(2,1)S(1)}, u32[]{:S(2)}, u32[]{:S(2)}) collective-permute-start(bf16[48,512]{1,0:T(8,128)(2,1)S(1)} %get-tuple-element.41.own_ref), channel_id=1, source_target_pairs={{0,192},{64,128},{128,64},{192,0},{1,193},{65,129},{129,65},{193,1... | collective-permute-start | bytes 147464 | tf_op jit(solution)/shard_map/ppermute | solution.py:408
  72.6 0.0 collective-permute-done.core_ref
  72.6 3.2 %collective-permute-done.1.side_ref = bf16[48,512]{1,0:T(8,128)(2,1)S(1)} collective-permute-done((bf16[48,512]{1,0:T(8,128)(2,1)S(1)}, bf16[48,512]{1,0:T(8,128)(2,1)S(1)}, u32[]{:S(2)}, u32[]{:S(2)}) %collective-permute-start.1) | collective-permute-done | bytes 49184 | tf_op jit(solution)/shard_map/ppermute | solution.py:407
  75.8 0.1 collective-permute-done.2.cross_ref
  75.9 6.1 %all-to-all-done.4.front_ref = bf16[64,8,128]{2,1,0:T(8,128)(2,1)S(1)} async-done(((bf16[64,8,128]{2,1,0:T(8,128)(2,1)}), bf16[64,8,128]{2,1,0:T(8,128)(2,1)S(1)}, u32[]{:S(2)}, u32[]{:S(2)}) %all-to-all-start.4) | async-done | bytes 131104 | tf_op jit(solution)/shard_map/all_to_all | solution.py:409
  82.0 0.7 last.1
  (2 shorter events, 0.0 us)
Async XLA Ops:
  0.6 9.9 %copy-start.4 = (s32[1024]{0:T(1024)S(1)}, s32[1024]{0:T(1024)}, u32[]{:S(2)}) copy-start(s32[1024]{0:T(1024)} %param.14) | copy-start | bytes 12292
  0.6 9.8 %copy-start = (s32[3,1024]{1,0:T(4,128)S(1)}, s32[3,1024]{1,0:T(4,128)}, u32[]{:S(2)}) copy-start(s32[3,1024]{1,0:T(4,128)} %connect_ref.3) | copy-start | bytes 36868
  0.7 9.8 %copy-start.1 = (bf16[3,512]{1,0:T(4,128)(2,1)S(1)}, bf16[3,512]{1,0:T(4,128)(2,1)}, u32[]{:S(2)}) copy-start(bf16[3,512]{1,0:T(4,128)(2,1)} %coords_ref.3) | copy-start | bytes 9220
  13.5 39.7 %copy-start.2 = (f32[1024]{0:T(1024)S(1)}, f32[1024]{0:T(1024)}, u32[]{:S(2)}) copy-start(f32[1024]{0:T(1024)} %param.11) | copy-start | bytes 12292
  13.5 39.7 %copy-start.3 = (s32[4,4]{1,0:T(4,128)S(1)}, s32[4,4]{1,0:T(4,128)}, u32[]{:S(2)}) copy-start(s32[4,4]{1,0:T(4,128)} %class_ref.1) | copy-start | bytes 196
  65.1 16.9 %all-to-all-start.4 = ((bf16[64,8,128]{2,1,0:T(8,128)(2,1)}), bf16[64,8,128]{2,1,0:T(8,128)(2,1)S(1)}, u32[]{:S(2)}, u32[]{:S(2)}) async-start(bf16[64,8,128]{2,1,0:T(8,128)(2,1)} %get-tuple-element.40), calls=%async_computation.4 | async-start | bytes 262144 | tf_op jit(solution)/shard_map/all_to_all | solution.py:409
  70.6 2.0 %collective-permute-start = (bf16[48,512]{1,0:T(8,128)(2,1)S(1)}, bf16[48,512]{1,0:T(8,128)(2,1)S(1)}, u32[]{:S(2)}, u32[]{:S(2)}) collective-permute-start(bf16[48,512]{1,0:T(8,128)(2,1)S(1)} %get-tuple-element.41.own_ref), channel_id=1, source_target_pairs={{0,64},{64,0},{128,192},{192,128},{1,65},{65,1},{129,193},{193,129... | collective-permute-start | bytes 147464 | tf_op jit(solution)/shard_map/ppermute | solution.py:406
  70.7 5.1 %collective-permute-start.1 = (bf16[48,512]{1,0:T(8,128)(2,1)S(1)}, bf16[48,512]{1,0:T(8,128)(2,1)S(1)}, u32[]{:S(2)}, u32[]{:S(2)}) collective-permute-start(bf16[48,512]{1,0:T(8,128)(2,1)S(1)} %get-tuple-element.41.own_ref), channel_id=1, source_target_pairs={{0,128},{64,192},{128,0},{192,64},{1,129},{65,193},{129,1},{193,65... | collective-permute-start | bytes 147464 | tf_op jit(solution)/shard_map/ppermute | solution.py:407
  71.3 4.6 %collective-permute-start.2 = (bf16[48,512]{1,0:T(8,128)(2,1)S(1)}, bf16[48,512]{1,0:T(8,128)(2,1)S(1)}, u32[]{:S(2)}, u32[]{:S(2)}) collective-permute-start(bf16[48,512]{1,0:T(8,128)(2,1)S(1)} %get-tuple-element.41.own_ref), channel_id=1, source_target_pairs={{0,192},{64,128},{128,64},{192,0},{1,193},{65,129},{129,65},{193,1... | collective-permute-start | bytes 147464 | tf_op jit(solution)/shard_map/ppermute | solution.py:408

commit v6 on v5

--- a/solution.py
+++ b/solution.py
@@ -227,11 +227,6 @@
         soften = jnp.where(class_ref[step // 16, jt] == 1, 3.0e38, SOFTEN).astype(F32)
         fill(kcell_ref, step, slice(256 * jt, 256 * jt + 256), 512, soften)
 
-    weave(
-        [lambda s=s, h=h: node_fill(s, h) for h in range(2) for s in range(64)],
-        [lambda jt=jt: part(jt) for jt in range(4)],
-    )
-
     def blend(step):
         at = slice(16 * step, 16 * step + 16)
         part = [part_ref[jt, at, :] for jt in range(4)]
@@ -255,33 +250,40 @@
         product = jnp.dot(fpack_ref[...], kcell_ref[k, :, lanes], preferred_element_type=F32)
         elem_ref[16 * k : 16 * k + 16, lanes] = load_sum(product * leader, 256)
 
-    weave(
-        [lambda s=s, jt=jt: cell_fill(s, jt) for jt in range(2) for s in range(64)],
-        [lambda s=s: blend(s) for s in range(18)]
-        + [lambda k=k, it=it: node_dot(k, it) for k in range(3) for it in range(4)]
-        + [lambda k=k: cell_dot(k, 0) for k in range(3)],
-    )
-
+    cells = [[] for it in range(4)]
     pieces = [[] for it in range(4)]
 
-    def row_dot(k, it):
+    def row_cell(k, it):
         rows = slice(256 * it, 256 * it + 256)
-        product = 3.0 * lax.dot_general(
-            share_ref[...], kcell_ref[k, rows, :], NT, preferred_element_type=F32
-        ) + lax.dot_general(nhalf_ref[it], knode_ref[k, rows, :], NT, preferred_element_type=F32)
-        pieces[it].append(-load_sum(product * fpack_ref[:, rows].astype(F32), 256))
+        product = lax.dot_general(share_ref[...], kcell_ref[k, rows, :], NT, preferred_element_type=F32)
+        cells[it].append(load_sum(product * fpack_ref[:, rows].astype(F32), 256))
+
+    def row_node(k, it):
+        rows = slice(256 * it, 256 * it + 256)
+        product = lax.dot_general(nhalf_ref[it], knode_ref[k, rows, :], NT, preferred_element_type=F32)
+        value = load_sum(product * fpack_ref[:, rows].astype(F32), 256)
+        pieces[it].append(-(value + 3.0 * cells[it][k]))
 
     for it in range(4):
         if it == 0:
-            few = [lambda k=k: cell_dot(k, 1) for k in range(3)]
+            few = [lambda jt=jt: part(jt) for jt in range(4)]
         else:
-            few = [lambda k=k, it=it: row_dot(k, it - 1) for k in range(3)]
-        weave([lambda s=s, jt=jt, it=it: cell_fill(16 * it + s, jt) for s in range(16) for jt in (2, 3)], few)
-    for k in range(3):
-        row_dot(k, 3)
-    for jt in (2, 3):
+            few = [lambda k=k, it=it: row_cell(k, it - 1) for k in range(3)]
+        weave([lambda s=s, jt=jt, it=it: cell_fill(16 * it + s, jt) for s in range(16) for jt in range(4)], few)
+    many = []
+    for s in range(64):
+        many += [lambda s=s, h=h: node_fill(s, h) for h in range(2)]
+        if s % 3 == 0 and s // 3 < 18:
+            many.append(lambda s=s: blend(s // 3))
+    weave(
+        many,
+        [lambda k=k: row_cell(k, 3) for k in range(3)]
+        + [lambda k=k, jt=jt: cell_dot(k, jt) for jt in range(4) for k in range(3)],
+    )
+    for it in range(4):
         for k in range(3):
-            cell_dot(k, jt)
+            node_dot(k, it)
+            row_node(k, it)
     nodes = jnp.concatenate([part[0] + part[1] + part[2] + part[3] for part in nodes], 0)
     value = elem_ref[...]
     high = value.astype(BF)

time: 83.1 us -> 82.2 us (0.989)
  Pallas kernels: 15.4 us -> 14.5 us
    pallas_call x1, Pallas kernels: 11.9 us -> 11 us  [body(): pl.pallas_call(main_kernel, out_shape=(shape((64, 8, 128), BF), shape((48...]
where the time goes in v6:
time: 82.2 us; the launch traced here: 81.8 us
  blocking collectives  47.2 us (57%)
  Pallas kernels  14.5 us (18%)
  waiting for transfers between devices  9.45 us (11%)
  starting transfers between devices  7.47 us (9%)
  other arithmetic  1.75 us (2%)
  between operations  1.36 us (2%)
    all_to_all x1, blocking collectives, compact(): return (lax.all_to_all(merged, ('yh', 'x'), 0, 0), place)  20 us
    all_to_all x1, blocking collectives, compact(): part = lax.all_to_all(pool, 'z', 0, 0)  19.3 us
    pallas_call x1, Pallas kernels, body(): pl.pallas_call(main_kernel, out_shape=(shape((64, 8, 128), BF), shape((48...  11 us
    all_gather x1, blocking collectives, body(): gathered = lax.all_gather(mine, ROW)  7.97 us
    all_to_all x1, waiting for transfers between devices, body(): front_sum = lax.all_to_all(front_part, COL, 0, 0)  6.12 us
    all_to_all x1, starting transfers between devices, body(): front_sum = lax.all_to_all(front_part, COL, 0, 0)  5.53 us
    ppermute x1, waiting for transfers between devices, body(): side = lax.ppermute(node_part, ROW, [(i, i ^ 2) for i in range(4)])  3.25 us
    pallas_call x1, Pallas kernels, body(): pl.pallas_call(prep_kernel, out_shape=(shape((288, 1024), BF), shape((16,...  2.32 us
  transfers between devices with their start and end apart: 4, of which 3 were waited for; matrix products, arithmetic and copies ran while one was open for 0% of the time, Pallas kernels for 0%

profile of v6, /device:TPU:2, one launch (start us, length us, event | category | flops | bytes accessed | tf_op | source)
XLA Modules:
  0.0 81.8 jit_solution(11437487925329597624)
XLA Ops:
  0.6 0.0 copy-start.4
  0.6 0.0 copy-start
  0.7 0.0 copy-start.1
  0.7 0.7 shift-right-arithmetic_convert_fusion
  1.4 0.1 pad.21.clone
  1.5 1.0 %maximum_maximum_fusion = bf16[80,1024]{1,0:T(8,128)(2,1)S(1)} fusion(bf16[1,1024]{1,0:T(2,128)(2,1)S(1)} %convert_element_type.19, bf16[36,1024]{1,0:T(8,128)(2,1)} %bitcast.31, bf16[36,1024]{1,0:T(8,128)(2,1)} %bitcast.32, bf16[80]{0:T(256)(128)(2,1)S(1)} %pad.21.clone), kind=kLoop, calls=%fused_computation.10 | loop fusion | flops 655360 | bytes 313504 | tf_op jit(solution)/shard_map/concatenate | solution.py:326
  2.5 8.0 %all-gather = bf16[320,1024]{1,0:T(8,128)(2,1)S(1)} all-gather(bf16[80,1024]{1,0:T(8,128)(2,1)S(1)} %maximum_maximum_fusion), channel_id=2, replica_groups=mesh['yl'=2,'co'=2,'z'=8,'yh'=2,'x'=4] {'yl','co'}, dimensions={0}, use_global_device_ids=true | all-gather | bytes 819200 | tf_op jit(solution)/shard_map/all_gather | solution.py:327
  10.5 0.0 copy-done.4
  10.5 0.0 copy-done
  10.5 0.0 copy-done.1
  10.5 2.3 %prep.1 = (bf16[288,1024]{1,0:T(8,128)(2,1)S(1)}, f32[16,1024]{1,0:T(8,128)S(1)}, bf16[304,1024]{1,0:T(8,128)(2,1)S(1)}, bf16[8,96,128]{2,1,0:T(8,128)(2,1)S(1)}, s32[2,1024]{1,0:T(2,128)S(1)}, /*index=5*/s32[1,1]{1,0:T(1,128)}) custom-call(s32[1]{0:T(128)} %bitcast.7.col_ref, bf16[4,80,1024]{2,1,0:T(8,128)(2,1)S(1)} %bitcast.24, s32[3,1024]{1,0:T(4,128)S(1)} %copy-done, ...), custom_call_target="tpu_custom_call" | custom-call | tf_op jit(solution)/shard_map/prep/pallas_call | solution.py:328
  13.5 0.0 copy-start.2
  13.5 0.0 copy-start.3
  13.5 39.7 %conditional.1 = (bf16[8,416,128]{2,1,0:T(8,128)(2,1)S(1)}, s32[2,1024]{1,0:T(2,128)S(1)}) conditional(s32[]{:T(128)} %bitcast.13, (s32[1]{0:T(128)}, bf16[304,1024]{1,0:T(8,128)(2,1)S(1)}, s32[1,1024]{1,0:T(1,128)S(1)}) %tuple.25, (bf16[8,96,128]{2,1,0:T(8,128)(2,1)S(1)}, s32[1]{0:T(128)}, s32[2,1024]{1,0:T(2,128)S(1)}) %tuple.17), branch_computations={%region_0.2_spmd, %region_2.3_spmd} | conditional | flops 3598336 | bytes 10766870 | solution.py:376
  13.5 19.3 %all_to_all.23.pool_ref = bf16[8,96,128]{2,1,0:T(8,128)(2,1)S(1)} all-to-all(bf16[8,96,128]{2,1,0:T(8,128)(2,1)S(1)} %get-tuple-element.16), channel_id=1, replica_groups=mesh['yl'=2,'co'=2,'z'=8,'yh'=2,'x'=4] {'z'}, dimensions={0} | all-to-all | bytes 393216 | tf_op jit(solution)/shard_map/cond/branch_1_fun/all_to_all | solution.py:345
  32.8 0.4 merge.1
  33.2 20.0 %all_to_all.24 = bf16[8,416,128]{2,1,0:T(8,128)(2,1)S(1)} all-to-all(bf16[8,416,128]{2,1,0:T(8,128)(2,1)S(1)} %merge.1), channel_id=1, replica_groups=mesh['yl'=2,'co'=2,'z'=8,'yh'=2,'x'=4] {'yh','x'}, dimensions={0} | all-to-all | bytes 1703936 | tf_op jit(solution)/shard_map/cond/branch_1_fun/all_to_all | solution.py:354
  53.1 0.0 copy-done.2
  53.1 0.0 copy-done.3
  53.1 11.0 %sweep.1 = (bf16[64,8,128]{2,1,0:T(8,128)(2,1)}, bf16[48,512]{1,0:T(8,128)(2,1)S(1)}) custom-call(s32[1]{0:T(128)} %bitcast.7.col_ref, s32[4,4]{1,0:T(4,128)S(1)} %copy-done.3, bf16[288,1024]{1,0:T(8,128)(2,1)S(1)} %get-tuple-element.32.pack_ref, f32[16,1024]{1,0:T(8,128)S(1)} %get-tuple-element.33.points_ref, f32[1,1024]{1,0:T(1,128)S(1)} %bitcast.25, ...), custom_call_target="tpu_custom_call" | custom-call | tf_op jit(solution)/shard_map/sweep/pallas_call | solution.py:377
  64.1 5.5 %all-to-all-start.4 = ((bf16[64,8,128]{2,1,0:T(8,128)(2,1)}), bf16[64,8,128]{2,1,0:T(8,128)(2,1)S(1)}, u32[]{:S(2)}, u32[]{:S(2)}) async-start(bf16[64,8,128]{2,1,0:T(8,128)(2,1)} %get-tuple-element.40), calls=%async_computation.4 | async-start | bytes 262144 | tf_op jit(solution)/shard_map/all_to_all | solution.py:411
  69.7 0.1 collective-permute-start
  69.8 0.6 collective-permute-start.1
  70.3 1.3 %collective-permute-start.2 = (bf16[48,512]{1,0:T(8,128)(2,1)S(1)}, bf16[48,512]{1,0:T(8,128)(2,1)S(1)}, u32[]{:S(2)}, u32[]{:S(2)}) collective-permute-start(bf16[48,512]{1,0:T(8,128)(2,1)S(1)} %get-tuple-element.41.own_ref), channel_id=1, source_target_pairs={{0,192},{64,128},{128,64},{192,0},{1,193},{65,129},{129,65},{193,1... | collective-permute-start | bytes 147464 | tf_op jit(solution)/shard_map/ppermute | solution.py:410
  71.6 0.0 collective-permute-done.core_ref
  71.6 3.2 %collective-permute-done.1.side_ref = bf16[48,512]{1,0:T(8,128)(2,1)S(1)} collective-permute-done((bf16[48,512]{1,0:T(8,128)(2,1)S(1)}, bf16[48,512]{1,0:T(8,128)(2,1)S(1)}, u32[]{:S(2)}, u32[]{:S(2)}) %collective-permute-start.1) | collective-permute-done | bytes 49184 | tf_op jit(solution)/shard_map/ppermute | solution.py:409
  74.9 0.1 collective-permute-done.2.cross_ref
  74.9 6.1 %all-to-all-done.4.front_ref = bf16[64,8,128]{2,1,0:T(8,128)(2,1)S(1)} async-done(((bf16[64,8,128]{2,1,0:T(8,128)(2,1)}), bf16[64,8,128]{2,1,0:T(8,128)(2,1)S(1)}, u32[]{:S(2)}, u32[]{:S(2)}) %all-to-all-start.4) | async-done | bytes 131104 | tf_op jit(solution)/shard_map/all_to_all | solution.py:411
  81.1 0.7 last.1
  (2 shorter events, 0.0 us)
Async XLA Ops:
  0.6 9.9 %copy-start.4 = (s32[1024]{0:T(1024)S(1)}, s32[1024]{0:T(1024)}, u32[]{:S(2)}) copy-start(s32[1024]{0:T(1024)} %param.14) | copy-start | bytes 12292
  0.6 9.8 %copy-start = (s32[3,1024]{1,0:T(4,128)S(1)}, s32[3,1024]{1,0:T(4,128)}, u32[]{:S(2)}) copy-start(s32[3,1024]{1,0:T(4,128)} %connect_ref.3) | copy-start | bytes 36868
  0.7 9.8 %copy-start.1 = (bf16[3,512]{1,0:T(4,128)(2,1)S(1)}, bf16[3,512]{1,0:T(4,128)(2,1)}, u32[]{:S(2)}) copy-start(bf16[3,512]{1,0:T(4,128)(2,1)} %coords_ref.3) | copy-start | bytes 9220
  13.5 39.7 %copy-start.2 = (f32[1024]{0:T(1024)S(1)}, f32[1024]{0:T(1024)}, u32[]{:S(2)}) copy-start(f32[1024]{0:T(1024)} %param.11) | copy-start | bytes 12292
  13.5 39.7 %copy-start.3 = (s32[4,4]{1,0:T(4,128)S(1)}, s32[4,4]{1,0:T(4,128)}, u32[]{:S(2)}) copy-start(s32[4,4]{1,0:T(4,128)} %class_ref.1) | copy-start | bytes 196
  64.1 16.9 %all-to-all-start.4 = ((bf16[64,8,128]{2,1,0:T(8,128)(2,1)}), bf16[64,8,128]{2,1,0:T(8,128)(2,1)S(1)}, u32[]{:S(2)}, u32[]{:S(2)}) async-start(bf16[64,8,128]{2,1,0:T(8,128)(2,1)} %get-tuple-element.40), calls=%async_computation.4 | async-start | bytes 262144 | tf_op jit(solution)/shard_map/all_to_all | solution.py:411
  69.7 2.0 %collective-permute-start = (bf16[48,512]{1,0:T(8,128)(2,1)S(1)}, bf16[48,512]{1,0:T(8,128)(2,1)S(1)}, u32[]{:S(2)}, u32[]{:S(2)}) collective-permute-start(bf16[48,512]{1,0:T(8,128)(2,1)S(1)} %get-tuple-element.41.own_ref), channel_id=1, source_target_pairs={{0,64},{64,0},{128,192},{192,128},{1,65},{65,1},{129,193},{193,129... | collective-permute-start | bytes 147464 | tf_op jit(solution)/shard_map/ppermute | solution.py:408
  69.8 5.1 %collective-permute-start.1 = (bf16[48,512]{1,0:T(8,128)(2,1)S(1)}, bf16[48,512]{1,0:T(8,128)(2,1)S(1)}, u32[]{:S(2)}, u32[]{:S(2)}) collective-permute-start(bf16[48,512]{1,0:T(8,128)(2,1)S(1)} %get-tuple-element.41.own_ref), channel_id=1, source_target_pairs={{0,128},{64,192},{128,0},{192,64},{1,129},{65,193},{129,1},{193,65... | collective-permute-start | bytes 147464 | tf_op jit(solution)/shard_map/ppermute | solution.py:409
  70.3 4.6 %collective-permute-start.2 = (bf16[48,512]{1,0:T(8,128)(2,1)S(1)}, bf16[48,512]{1,0:T(8,128)(2,1)S(1)}, u32[]{:S(2)}, u32[]{:S(2)}) collective-permute-start(bf16[48,512]{1,0:T(8,128)(2,1)S(1)} %get-tuple-element.41.own_ref), channel_id=1, source_target_pairs={{0,192},{64,128},{128,64},{192,0},{1,193},{65,129},{129,65},{193,1... | collective-permute-start | bytes 147464 | tf_op jit(solution)/shard_map/ppermute | solution.py:410

commit v7 on v6

--- a/solution.py
+++ b/solution.py
@@ -168,9 +168,6 @@
         hit = (node == ends[0]) | (node == ends[1]) | (node == ends[2])
         touch_ref[16 * step : 16 * step + 16, :] = one_hot(hit)
 
-    for step in range(32):
-        mark(step)
-
     pool = jnp.transpose(unfold(pool_ref[...], 8, SLOTS, SLOT_PART))[:304]
     chosen = one_hot(iota((8 * SLOTS, 1024), 0) == slot_ref[1:2, :])
     found = jnp.dot(pool, chosen, preferred_element_type=F32)
@@ -265,12 +262,9 @@
         pieces[it].append(-(value + 3.0 * cells[it][k]))
 
     for it in range(4):
-        if it == 0:
-            few = [lambda jt=jt: part(jt) for jt in range(4)]
-        else:
-            few = [lambda k=k, it=it: row_cell(k, it - 1) for k in range(3)]
+        few = [lambda k=k, it=it: row_cell(k, it - 1) for k in range(3)] if it else []
         weave([lambda s=s, jt=jt, it=it: cell_fill(16 * it + s, jt) for s in range(16) for jt in range(4)], few)
-    many = []
+    many = [lambda s=s: mark(s) for s in range(32)] + [lambda jt=jt: part(jt) for jt in range(4)]
     for s in range(64):
         many += [lambda s=s, h=h: node_fill(s, h) for h in range(2)]
         if s % 3 == 0 and s // 3 < 18:

time: 82.2 us -> 81.9 us (level)
  no operation moved by 1% of the time
where the time goes in v7:
time: 81.9 us; the launch traced here: 81.5 us
  blocking collectives  47.2 us (58%)
  Pallas kernels  14.2 us (17%)
  waiting for transfers between devices  9.44 us (12%)
  starting transfers between devices  7.48 us (9%)
  other arithmetic  1.75 us (2%)
  between operations  1.36 us (2%)
    all_to_all x1, blocking collectives, compact(): return (lax.all_to_all(merged, ('yh', 'x'), 0, 0), place)  20 us
    all_to_all x1, blocking collectives, compact(): part = lax.all_to_all(pool, 'z', 0, 0)  19.3 us
    pallas_call x1, Pallas kernels, body(): pl.pallas_call(main_kernel, out_shape=(shape((64, 8, 128), BF), shape((48...  10.7 us
    all_gather x1, blocking collectives, body(): gathered = lax.all_gather(mine, ROW)  7.97 us
    all_to_all x1, waiting for transfers between devices, body(): front_sum = lax.all_to_all(front_part, COL, 0, 0)  6.11 us
    all_to_all x1, starting transfers between devices, body(): front_sum = lax.all_to_all(front_part, COL, 0, 0)  5.54 us
    ppermute x1, waiting for transfers between devices, body(): side = lax.ppermute(node_part, ROW, [(i, i ^ 2) for i in range(4)])  3.25 us
    pallas_call x1, Pallas kernels, body(): pl.pallas_call(prep_kernel, out_shape=(shape((288, 1024), BF), shape((16,...  2.32 us
  transfers between devices with their start and end apart: 4, of which 3 were waited for; matrix products, arithmetic and copies ran while one was open for 0% of the time, Pallas kernels for 0%

profile of v7, /device:TPU:2, one launch (start us, length us, event | category | flops | bytes accessed | tf_op | source)
XLA Modules:
  0.0 81.5 jit_solution(2499333060251520615)
XLA Ops:
  0.6 0.0 copy-start.4
  0.6 0.0 copy-start
  0.7 0.0 copy-start.1
  0.7 0.7 shift-right-arithmetic_convert_fusion
  1.4 0.1 pad.21.clone
  1.5 1.0 %maximum_maximum_fusion = bf16[80,1024]{1,0:T(8,128)(2,1)S(1)} fusion(bf16[1,1024]{1,0:T(2,128)(2,1)S(1)} %convert_element_type.19, bf16[36,1024]{1,0:T(8,128)(2,1)} %bitcast.31, bf16[36,1024]{1,0:T(8,128)(2,1)} %bitcast.32, bf16[80]{0:T(256)(128)(2,1)S(1)} %pad.21.clone), kind=kLoop, calls=%fused_computation.10 | loop fusion | flops 655360 | bytes 313504 | tf_op jit(solution)/shard_map/concatenate | solution.py:320
  2.5 8.0 %all-gather = bf16[320,1024]{1,0:T(8,128)(2,1)S(1)} all-gather(bf16[80,1024]{1,0:T(8,128)(2,1)S(1)} %maximum_maximum_fusion), channel_id=2, replica_groups=mesh['yl'=2,'co'=2,'z'=8,'yh'=2,'x'=4] {'yl','co'}, dimensions={0}, use_global_device_ids=true | all-gather | bytes 819200 | tf_op jit(solution)/shard_map/all_gather | solution.py:321
  10.5 0.0 copy-done.4
  10.5 0.0 copy-done
  10.5 0.0 copy-done.1
  10.5 2.3 %prep.1 = (bf16[288,1024]{1,0:T(8,128)(2,1)S(1)}, f32[16,1024]{1,0:T(8,128)S(1)}, bf16[304,1024]{1,0:T(8,128)(2,1)S(1)}, bf16[8,96,128]{2,1,0:T(8,128)(2,1)S(1)}, s32[2,1024]{1,0:T(2,128)S(1)}, /*index=5*/s32[1,1]{1,0:T(1,128)}) custom-call(s32[1]{0:T(128)} %bitcast.7.col_ref, bf16[4,80,1024]{2,1,0:T(8,128)(2,1)S(1)} %bitcast.24, s32[3,1024]{1,0:T(4,128)S(1)} %copy-done, ...), custom_call_target="tpu_custom_call" | custom-call | tf_op jit(solution)/shard_map/prep/pallas_call | solution.py:322
  13.5 0.0 copy-start.2
  13.5 0.0 copy-start.3
  13.5 39.7 %conditional.1 = (bf16[8,416,128]{2,1,0:T(8,128)(2,1)S(1)}, s32[2,1024]{1,0:T(2,128)S(1)}) conditional(s32[]{:T(128)} %bitcast.13, (s32[1]{0:T(128)}, bf16[304,1024]{1,0:T(8,128)(2,1)S(1)}, s32[1,1024]{1,0:T(1,128)S(1)}) %tuple.25, (bf16[8,96,128]{2,1,0:T(8,128)(2,1)S(1)}, s32[1]{0:T(128)}, s32[2,1024]{1,0:T(2,128)S(1)}) %tuple.17), branch_computations={%region_0.2_spmd, %region_2.3_spmd} | conditional | flops 3598336 | bytes 10766870 | solution.py:370
  13.5 19.3 %all_to_all.23.pool_ref = bf16[8,96,128]{2,1,0:T(8,128)(2,1)S(1)} all-to-all(bf16[8,96,128]{2,1,0:T(8,128)(2,1)S(1)} %get-tuple-element.16), channel_id=1, replica_groups=mesh['yl'=2,'co'=2,'z'=8,'yh'=2,'x'=4] {'z'}, dimensions={0} | all-to-all | bytes 393216 | tf_op jit(solution)/shard_map/cond/branch_1_fun/all_to_all | solution.py:339
  32.8 0.4 merge.1
  33.2 20.0 %all_to_all.24 = bf16[8,416,128]{2,1,0:T(8,128)(2,1)S(1)} all-to-all(bf16[8,416,128]{2,1,0:T(8,128)(2,1)S(1)} %merge.1), channel_id=1, replica_groups=mesh['yl'=2,'co'=2,'z'=8,'yh'=2,'x'=4] {'yh','x'}, dimensions={0} | all-to-all | bytes 1703936 | tf_op jit(solution)/shard_map/cond/branch_1_fun/all_to_all | solution.py:348
  53.1 0.0 copy-done.2
  53.1 0.0 copy-done.3
  53.1 10.7 %sweep.1 = (bf16[64,8,128]{2,1,0:T(8,128)(2,1)}, bf16[48,512]{1,0:T(8,128)(2,1)S(1)}) custom-call(s32[1]{0:T(128)} %bitcast.7.col_ref, s32[4,4]{1,0:T(4,128)S(1)} %copy-done.3, bf16[288,1024]{1,0:T(8,128)(2,1)S(1)} %get-tuple-element.32.pack_ref, f32[16,1024]{1,0:T(8,128)S(1)} %get-tuple-element.33.points_ref, f32[1,1024]{1,0:T(1,128)S(1)} %bitcast.25, ...), custom_call_target="tpu_custom_call" | custom-call | tf_op jit(solution)/shard_map/sweep/pallas_call | solution.py:371
  63.9 5.5 %all-to-all-start.4 = ((bf16[64,8,128]{2,1,0:T(8,128)(2,1)}), bf16[64,8,128]{2,1,0:T(8,128)(2,1)S(1)}, u32[]{:S(2)}, u32[]{:S(2)}) async-start(bf16[64,8,128]{2,1,0:T(8,128)(2,1)} %get-tuple-element.40), calls=%async_computation.4 | async-start | bytes 262144 | tf_op jit(solution)/shard_map/all_to_all | solution.py:405
  69.4 0.1 collective-permute-start
  69.5 0.6 collective-permute-start.1
  70.1 1.3 %collective-permute-start.2 = (bf16[48,512]{1,0:T(8,128)(2,1)S(1)}, bf16[48,512]{1,0:T(8,128)(2,1)S(1)}, u32[]{:S(2)}, u32[]{:S(2)}) collective-permute-start(bf16[48,512]{1,0:T(8,128)(2,1)S(1)} %get-tuple-element.41.own_ref), channel_id=1, source_target_pairs={{0,192},{64,128},{128,64},{192,0},{1,193},{65,129},{129,65},{193,1... | collective-permute-start | bytes 147464 | tf_op jit(solution)/shard_map/ppermute | solution.py:404
  71.4 0.0 collective-permute-done.core_ref
  71.4 3.2 %collective-permute-done.1.side_ref = bf16[48,512]{1,0:T(8,128)(2,1)S(1)} collective-permute-done((bf16[48,512]{1,0:T(8,128)(2,1)S(1)}, bf16[48,512]{1,0:T(8,128)(2,1)S(1)}, u32[]{:S(2)}, u32[]{:S(2)}) %collective-permute-start.1) | collective-permute-done | bytes 49184 | tf_op jit(solution)/shard_map/ppermute | solution.py:403
  74.6 0.1 collective-permute-done.2.cross_ref
  74.7 6.1 %all-to-all-done.4.front_ref = bf16[64,8,128]{2,1,0:T(8,128)(2,1)S(1)} async-done(((bf16[64,8,128]{2,1,0:T(8,128)(2,1)}), bf16[64,8,128]{2,1,0:T(8,128)(2,1)S(1)}, u32[]{:S(2)}, u32[]{:S(2)}) %all-to-all-start.4) | async-done | bytes 131104 | tf_op jit(solution)/shard_map/all_to_all | solution.py:405
  80.8 0.7 last.1
  (2 shorter events, 0.0 us)
Async XLA Ops:
  0.6 9.9 %copy-start.4 = (s32[1024]{0:T(1024)S(1)}, s32[1024]{0:T(1024)}, u32[]{:S(2)}) copy-start(s32[1024]{0:T(1024)} %param.14) | copy-start | bytes 12292
  0.6 9.8 %copy-start = (s32[3,1024]{1,0:T(4,128)S(1)}, s32[3,1024]{1,0:T(4,128)}, u32[]{:S(2)}) copy-start(s32[3,1024]{1,0:T(4,128)} %connect_ref.3) | copy-start | bytes 36868
  0.7 9.8 %copy-start.1 = (bf16[3,512]{1,0:T(4,128)(2,1)S(1)}, bf16[3,512]{1,0:T(4,128)(2,1)}, u32[]{:S(2)}) copy-start(bf16[3,512]{1,0:T(4,128)(2,1)} %coords_ref.3) | copy-start | bytes 9220
  13.5 39.7 %copy-start.2 = (f32[1024]{0:T(1024)S(1)}, f32[1024]{0:T(1024)}, u32[]{:S(2)}) copy-start(f32[1024]{0:T(1024)} %param.11) | copy-start | bytes 12292
  13.5 39.7 %copy-start.3 = (s32[4,4]{1,0:T(4,128)S(1)}, s32[4,4]{1,0:T(4,128)}, u32[]{:S(2)}) copy-start(s32[4,4]{1,0:T(4,128)} %class_ref.1) | copy-start | bytes 196
  63.9 16.9 %all-to-all-start.4 = ((bf16[64,8,128]{2,1,0:T(8,128)(2,1)}), bf16[64,8,128]{2,1,0:T(8,128)(2,1)S(1)}, u32[]{:S(2)}, u32[]{:S(2)}) async-start(bf16[64,8,128]{2,1,0:T(8,128)(2,1)} %get-tuple-element.40), calls=%async_computation.4 | async-start | bytes 262144 | tf_op jit(solution)/shard_map/all_to_all | solution.py:405
  69.4 2.0 %collective-permute-start = (bf16[48,512]{1,0:T(8,128)(2,1)S(1)}, bf16[48,512]{1,0:T(8,128)(2,1)S(1)}, u32[]{:S(2)}, u32[]{:S(2)}) collective-permute-start(bf16[48,512]{1,0:T(8,128)(2,1)S(1)} %get-tuple-element.41.own_ref), channel_id=1, source_target_pairs={{0,64},{64,0},{128,192},{192,128},{1,65},{65,1},{129,193},{193,129... | collective-permute-start | bytes 147464 | tf_op jit(solution)/shard_map/ppermute | solution.py:402
  69.5 5.1 %collective-permute-start.1 = (bf16[48,512]{1,0:T(8,128)(2,1)S(1)}, bf16[48,512]{1,0:T(8,128)(2,1)S(1)}, u32[]{:S(2)}, u32[]{:S(2)}) collective-permute-start(bf16[48,512]{1,0:T(8,128)(2,1)S(1)} %get-tuple-element.41.own_ref), channel_id=1, source_target_pairs={{0,128},{64,192},{128,0},{192,64},{1,129},{65,193},{129,1},{193,65... | collective-permute-start | bytes 147464 | tf_op jit(solution)/shard_map/ppermute | solution.py:403
  70.1 4.6 %collective-permute-start.2 = (bf16[48,512]{1,0:T(8,128)(2,1)S(1)}, bf16[48,512]{1,0:T(8,128)(2,1)S(1)}, u32[]{:S(2)}, u32[]{:S(2)}) collective-permute-start(bf16[48,512]{1,0:T(8,128)(2,1)S(1)} %get-tuple-element.41.own_ref), channel_id=1, source_target_pairs={{0,192},{64,128},{128,64},{192,0},{1,193},{65,129},{129,65},{193,1... | collective-permute-start | bytes 147464 | tf_op jit(solution)/shard_map/ppermute | solution.py:404
